TPU v7x, 128 devices: a whole 4x4x4 slice. The times are simulated.
128 devices in a mesh: occ: 32 (over x, z, core), rep: 4 (over y).
Axes of the slice: x: 4, y: 4, z: 4, core: 2. Of those that a mesh axis runs over, the one named last changes fastest.
Arguments:
- coeffs: bfloat16 [512, 12, 64, 128], P(('occ', 'rep')), may hold values from -1 to 1
- amplitudes: bfloat16 [512, 4096], P(('occ', 'rep')), may hold values from -6 to 6
- denominators: float32 [512, 64], P(('occ', 'rep')), may hold values from 0.25 to 2
- pno_count: int32 [512], P(('occ', 'rep')), may hold values from 24 to 64
- domains: int32 [512, 12], replicated, may hold values from 0 to 31, as said below
- far_owner: int32 [512, 2], P(('occ', 'rep')), may hold values from 0 to 31, all different within a row; in each aligned block of 4 rows (0 to 3, 4 to 7, ...) at most 2 rows name the same one
- far_pair: int32 [512, 2], P(('occ', 'rep')), may hold values from 0 to 3
- near_pair: int32 [512, 40], P(('occ', 'rep')), may hold values from 0 to 15
Outputs:
- residual: float32 [512, 4096], P(('occ', 'rep'))
Inputs may be any that keep to these rules, and one draw needn't show every extreme that they name: `domains`: each row names 12 different blocks. `far_owner`: the 2 entries of a row differ; among the rows of one device no occupied block is named more than 2 times, and that bound is reached.
All inputs are finite; a program needn't handle non-finite values.
Results may differ from a plain program's by a relative error of at most 0.0003.
Values may be sent and summed in bfloat16 or wider, within the bound.
A program may use at most 128 MiB of HBM per device.

v0:
```python
import jax
import jax.numpy as jnp
from jax import lax
from jax.sharding import PartitionSpec as P

NPNO = 64
KN = 2


def intersection(left_coeff, left_dom, right_coeff, right_dom):
    matches = (left_dom[:, None] == right_dom[None, :]).astype(jnp.bfloat16)
    flat = right_coeff.reshape(right_coeff.shape[0], -1)
    aligned = (
        jnp.dot(matches, flat, preferred_element_type=jnp.float32)
        .astype(jnp.bfloat16)
        .reshape(right_coeff.shape)
    )
    per_block = jnp.einsum("arc,asc->ars", left_coeff, aligned, preferred_element_type=jnp.float32)
    return jnp.sum(per_block, axis=0)


def square_amps(amplitude):
    return amplitude.reshape(amplitude.shape[0], NPNO, NPNO).astype(jnp.float32)


def carry_each(intersections, amplitude):
    return jnp.einsum(
        "kab,kbc,kdc->kad",
        intersections,
        square_amps(amplitude),
        intersections,
        precision=lax.Precision.HIGHEST,
    )


def carry_back(intersections, amplitude):
    return jnp.einsum(
        "kba,kbc,kcd->kad",
        intersections,
        square_amps(amplitude),
        intersections,
        precision=lax.Precision.HIGHEST,
    )


def on_device(coeffs, amplitudes, denominators, pno_count, domains, far_owner, far_pair, near_pair):
    pair_count = coeffs.shape[0]
    occ_count = lax.axis_size("occ")
    rep_count = lax.axis_size("rep")
    capacity = max(2, 2 * pair_count * KN // occ_count)
    occ_index = lax.axis_index("occ")
    rep_index = lax.axis_index("rep")
    device = occ_index * rep_count + rep_index
    live_rows = jnp.arange(NPNO, dtype=jnp.int32)[None, :] < pno_count[:, None]
    live_both = live_rows[:, :, None] & live_rows[:, None, :]
    coeff_masked = jnp.where(live_rows[:, None, :, None], coeffs, jnp.zeros((), jnp.bfloat16))
    amp_masked = jnp.where(
        live_both.reshape(pair_count, -1), amplitudes, jnp.zeros((), jnp.bfloat16)
    )
    home_dom = lax.dynamic_slice_in_dim(domains, device * pair_count, pair_count, 0)
    group_coeff, group_amp = (
        lax.all_gather(coeff_masked, "rep", axis=0, tiled=True),
        lax.all_gather(amp_masked, "rep", axis=0, tiled=True),
    )
    group_dom = lax.dynamic_slice_in_dim(
        domains, occ_index * rep_count * pair_count, rep_count * pair_count, 0
    )

    def near_term(operands):
        left_coeff, left_dom, chosen = operands
        intersections = jax.vmap(intersection, in_axes=(None, None, 0, 0))(
            left_coeff, left_dom, group_coeff[chosen], group_dom[chosen]
        )
        return jnp.sum(carry_each(intersections, group_amp[chosen]), axis=0)

    near_gain = lax.map(near_term, (coeff_masked, home_dom, near_pair))
    owner_flat = far_owner.reshape(-1)
    pair_flat = far_pair.reshape(-1)
    request_total = owner_flat.shape[0]
    source_pair = jnp.repeat(jnp.arange(pair_count, dtype=jnp.int32), KN)
    owner_hot = (owner_flat[:, None] == jnp.arange(occ_count, dtype=jnp.int32)[None, :]).astype(
        jnp.int32
    )
    earlier = jnp.cumsum(owner_hot, axis=0) - owner_hot
    slot_index = jnp.sum(earlier * owner_hot, axis=1)
    slot_hot = (slot_index[:, None] == jnp.arange(capacity, dtype=jnp.int32)[None, :]).astype(
        jnp.int32
    )
    position = owner_flat * capacity + slot_index
    slot_total = occ_count * capacity
    block_shape = coeffs.shape[1:]
    far_ids = (owner_flat * rep_count + rep_index) * pair_count + pair_flat
    asked_for = lax.all_to_all(
        jnp.einsum("rd,rs->ds", owner_hot * (pair_flat + 1)[:, None], slot_hot),
        "occ",
        split_axis=0,
        concat_axis=0,
        tiled=True,
    )
    wanted = jnp.maximum(asked_for - 1, 0)
    filled = asked_for > 0
    send_coeff = jnp.where(
        filled[:, :, None, None, None], coeff_masked[wanted], jnp.zeros((), jnp.bfloat16)
    )
    send_amps = jnp.where(filled[:, :, None], amp_masked[wanted], jnp.zeros((), jnp.bfloat16))
    recv_coeff, recv_amps = (
        lax.all_to_all(send_coeff, "occ", split_axis=0, concat_axis=0, tiled=True),
        lax.all_to_all(send_amps, "occ", split_axis=0, concat_axis=0, tiled=True),
    )
    far_coeff = recv_coeff.reshape((slot_total,) + block_shape)[position]
    far_amps = recv_amps.reshape(slot_total, -1)[position]
    intersections = jax.vmap(intersection)(
        coeff_masked[source_pair], home_dom[source_pair], far_coeff, domains[far_ids]
    )
    far_gain = carry_each(intersections, far_amps).reshape(pair_count, KN, NPNO, NPNO).sum(axis=1)
    back_terms = carry_back(intersections, amp_masked[source_pair]).reshape(request_total, -1)
    outgoing = jnp.zeros((slot_total, NPNO * NPNO), jnp.float32).at[position].set(back_terms)
    returned = lax.all_to_all(
        outgoing.reshape(occ_count, capacity, -1), "occ", split_axis=0, concat_axis=0, tiled=True
    )
    receivers = asked_for.reshape(-1) - 1
    owner_table = (jnp.arange(pair_count, dtype=jnp.int32)[:, None] == receivers[None, :]).astype(
        jnp.float32
    )
    back_sum = jnp.dot(
        owner_table, returned.reshape(slot_total, -1), precision=lax.Precision.HIGHEST
    )
    denominator_sum = denominators[:, :, None] + denominators[:, None, :]
    residual = (
        denominator_sum * square_amps(amp_masked)
        + near_gain
        + far_gain
        + back_sum.reshape(pair_count, NPNO, NPNO)
    )
    residual = jnp.where(live_both, residual, jnp.zeros((), jnp.float32))
    return residual.reshape(pair_count, NPNO * NPNO)


def solution(mesh):
    in_specs = (
        P(("occ", "rep"), None, None, None),
        P(("occ", "rep"), None),
        P(("occ", "rep"), None),
        P(("occ", "rep")),
        P(),
        P(("occ", "rep"), None),
        P(("occ", "rep"), None),
        P(("occ", "rep"), None),
    )
    out_specs = P(("occ", "rep"), None)
    return jax.shard_map(
        on_device, mesh=mesh, in_specs=in_specs, out_specs=out_specs, check_vma=False
    )
```

profile of v0, /device:TPU:1, one launch (start us, length us, event | category | flops | bytes accessed | tf_op | source)
XLA Modules:
  0.0 541.6 jit_solution(10062439628846564984)
XLA Ops:
  9.4 9.4 %all-to-all-start = ((s32[32,1,2]{2,1,0:T(1,128)}), s32[32,1,2]{2,1,0:T(1,128)S(1)}, u32[]{:S(2)}, u32[]{:S(2)}) async-start(s32[32,1,2]{2,1,0:T(1,128)} %bitcast.28), calls=%async_computation | async-start | bytes 32768 | tf_op jit(solution)/shard_map/all_to_all | solution.py:93
  22.7 3.1 all-to-all-done
  28.8 4.3 all-to-all-start.1
  33.1 6.9 %gather_fusion.8 = bf16[64,12,64,128]{3,2,1,0:T(8,128)(2,1)} fusion(bf16[4,12,64,128]{3,2,1,0:T(8,128)(2,1)S(1)} %broadcast_select_fusion.2, s32[1024]{0:T(1024)S(1)} %pad_clamp_fusion.4), kind=kCustom, calls=%fused_computation.8 | custom fusion | bytes 25166080 | tf_op jit(solution)/shard_map/gather | solution.py:103
  39.9 10.7 %broadcast_select_fusion = bf16[32,2,12,64,128]{4,3,2,1,0:T(8,128)(2,1)} fusion(bf16[32,2,12,64,128]{4,3,2,1,0:T(8,128)(2,1)} %bitcast.109, pred[32,2]{1,0:T(8,128)(4,1)S(1)} %copy.135), kind=kLoop, calls=%fused_computation.27 | loop fusion | flops 6291456 | bytes 25165888 | tf_op jit(solution)/shard_map/jit(_where)/select_n | solution.py:102
  50.6 7.4 %all-to-all-start.2 = ((bf16[32,2,12,64,128]{4,3,2,1,0:T(8,128)(2,1)}), bf16[32,2,12,64,128]{4,3,2,1,0:T(8,128)(2,1)}, u32[]{:S(2)}, u32[]{:S(2)}) async-start(bf16[32,2,12,64,128]{4,3,2,1,0:T(8,128)(2,1)} %broadcast_select_fusion), calls=%async_computation.2 | async-start | bytes 25165824 | tf_op jit(solution)/shard_map/all_to_all | solution.py:107
  60.5 2.0 gather_fusion.5
  63.6 10.9 %all-gather = bf16[4,4,4096]{2,1,0:T(4,128)(2,1)S(1)} all-gather(bf16[1,4,4096]{2,1,0:T(4,128)(2,1)S(1)} %bitcast.108), channel_id=1, replica_groups=mesh['occ'=32,'rep'=4] {'rep'}, dimensions={0}, use_global_device_ids=true | all-gather | bytes 163840 | tf_op jit(solution)/shard_map/all_gather | solution.py:63
  78.1 155.1 %all-to-all-done.2 = bf16[32,2,12,64,128]{4,3,2,1,0:T(8,128)(2,1)} async-done(((bf16[32,2,12,64,128]{4,3,2,1,0:T(8,128)(2,1)}), bf16[32,2,12,64,128]{4,3,2,1,0:T(8,128)(2,1)}, u32[]{:S(2)}, u32[]{:S(2)}) %all-to-all-start.2) | async-done | bytes 12582944 | tf_op jit(solution)/shard_map/all_to_all | solution.py:107
  233.2 6.5 %gather_fusion.9 = bf16[8,12,64,128]{3,2,1,0:T(8,128)(2,1)} fusion(bf16[64,12,64,128]{3,2,1,0:T(8,128)(2,1)} %bitcast.18, s32[1024]{0:T(1024)S(1)} %pad_clamp_fusion.3), kind=kCustom, calls=%fused_computation.9 | custom fusion | bytes 3145760 | tf_op jit(solution)/shard_map/gather | solution.py:110
  239.7 2.7 reshape.418
  242.4 2.1 convolution_convert_fusion.1
  244.5 3.0 reshape.419
  247.5 2.0 convolution_bitcast_fusion.1
  251.3 1.6 reshape.305
  252.9 27.7 %all-to-all-start.3 = ((f32[32,2,4096]{2,1,0:T(2,128)}), f32[32,2,4096]{2,1,0:T(2,128)}, u32[]{:S(2)}, u32[]{:S(2)}) async-start(f32[32,2,4096]{2,1,0:T(2,128)} %reshape.305), calls=%async_computation.3 | async-start | bytes 2097152 | tf_op jit(solution)/shard_map/all_to_all | solution.py:118
  280.6 244.6 %while.11 = (s32[]{:T(128)}, f32[4,64,64]{2,0,1:T(4,128)}, s32[4,40]{1,0:T(4,128)}, bf16[16,4096]{1,0:T(8,128)(2,1)S(1)}, bf16[4,12,64,128]{3,2,1,0:T(8,128)(2,1...) while((s32[]{:T(128)}, f32[4,64,64]{2,0,1:T(4,128)}, ...), condition=%wide.region_1.2_spmd.clone, body=%wide.region_0.1_spmd.sunk.clone | while | flops 853285632 | bytes 92998288 | solution.py:76
  283.3 1.5 gather_fusion
  284.8 2.5 reshape.458
  287.3 5.9 %gather_fusion.1 = bf16[40,12,64,128]{3,2,1,0:T(8,128)(2,1)} fusion(bf16[16,12,64,128]{3,2,1,0:T(8,128)(2,1)S(1)} %copy-done, s32[1024]{0:T(1024)S(1)} %pad_clamp_fusion.7), kind=kCustom, calls=%fused_computation.2.clone.1.clone | custom fusion | bytes 15728800 | tf_op jit(solution)/shard_map/while/body/eval_jaxpr/gather | solution.py:72
  293.2 13.3 %reshape.459 = bf16[40,12,8192]{2,1,0:T(8,128)(2,1)} reshape(bf16[40,12,64,128]{3,2,1,0:T(8,128)(2,1)} %gather_fusion.1) | data formatting | bytes 15728640 | tf_op jit(solution)/shard_map/while/body/eval_jaxpr/vmap()/reshape | solution.py:12
  306.5 10.7 %convolution_convert_fusion.4 = bf16[40,12,8192]{2,1,0:T(8,128)(2,1)} fusion(bf16[40,12,8192]{2,1,0:T(8,128)(2,1)} %reshape.459, s32[40,12]{1,0:T(8,128)S(1)} %copy-done.5, s32[12]{0:T(128)S(1)} %copy-done.12), kind=kOutput, calls=%fused_computation.12.clone.1.clone | convolution fusion | flops 98309760 | bytes 15730608 | tf_op jit(solution)/shard_map/while/body/eval_jaxpr/vmap()/dot_general | solution.py:14
  317.2 13.7 %reshape.460 = bf16[40,12,64,128]{3,2,1,0:T(8,128)(2,1)} reshape(bf16[40,12,8192]{2,1,0:T(8,128)(2,1)} %convolution_convert_fusion.4) | data formatting | bytes 15728640 | tf_op jit(solution)/shard_map/while/body/eval_jaxpr/vmap()/reshape | solution.py:16
  330.9 7.1 %convolution_bitcast_fusion.4 = f32[40,64,64]{2,1,0:T(8,128)S(1)} fusion(bf16[40,12,64,128]{3,2,1,0:T(8,128)(2,1)} %reshape.460, bf16[4,12,64,128]{3,2,1,0:T(8,128)(2,1)S(1)} %copy-done.3, s32[]{:T(128)S(6)} %copy.177), kind=kOutput, calls=%fused_computation.13.clone.1.clone | convolution fusion | flops 503316480 | bytes 8716292 | tf_op jit(solution)/shard_map/while/body/eval_jaxpr/vmap(arc,asc->ars)/dot_general | solution.py:18
  340.1 1.7 dynamic_update_slice.6
  346.0 2.5 reshape.458
  348.4 5.9 %gather_fusion.1 = bf16[40,12,64,128]{3,2,1,0:T(8,128)(2,1)} fusion(bf16[16,12,64,128]{3,2,1,0:T(8,128)(2,1)S(1)} %copy-done, s32[1024]{0:T(1024)S(1)} %pad_clamp_fusion.7), kind=kCustom, calls=%fused_computation.2.clone.1.clone | custom fusion | bytes 15728800 | tf_op jit(solution)/shard_map/while/body/eval_jaxpr/gather | solution.py:72
  354.3 13.3 %reshape.459 = bf16[40,12,8192]{2,1,0:T(8,128)(2,1)} reshape(bf16[40,12,64,128]{3,2,1,0:T(8,128)(2,1)} %gather_fusion.1) | data formatting | bytes 15728640 | tf_op jit(solution)/shard_map/while/body/eval_jaxpr/vmap()/reshape | solution.py:12
  367.6 10.7 %convolution_convert_fusion.4 = bf16[40,12,8192]{2,1,0:T(8,128)(2,1)} fusion(bf16[40,12,8192]{2,1,0:T(8,128)(2,1)} %reshape.459, s32[40,12]{1,0:T(8,128)S(1)} %copy-done.5, s32[12]{0:T(128)S(1)} %copy-done.12), kind=kOutput, calls=%fused_computation.12.clone.1.clone | convolution fusion | flops 98309760 | bytes 15730608 | tf_op jit(solution)/shard_map/while/body/eval_jaxpr/vmap()/dot_general | solution.py:14
  378.4 13.7 %reshape.460 = bf16[40,12,64,128]{3,2,1,0:T(8,128)(2,1)} reshape(bf16[40,12,8192]{2,1,0:T(8,128)(2,1)} %convolution_convert_fusion.4) | data formatting | bytes 15728640 | tf_op jit(solution)/shard_map/while/body/eval_jaxpr/vmap()/reshape | solution.py:16
  392.1 7.1 %convolution_bitcast_fusion.4 = f32[40,64,64]{2,1,0:T(8,128)S(1)} fusion(bf16[40,12,64,128]{3,2,1,0:T(8,128)(2,1)} %reshape.460, bf16[4,12,64,128]{3,2,1,0:T(8,128)(2,1)S(1)} %copy-done.3, s32[]{:T(128)S(6)} %copy.177), kind=kOutput, calls=%fused_computation.13.clone.1.clone | convolution fusion | flops 503316480 | bytes 8716292 | tf_op jit(solution)/shard_map/while/body/eval_jaxpr/vmap(arc,asc->ars)/dot_general | solution.py:18
  401.3 1.7 dynamic_update_slice.6
  407.1 2.5 reshape.458
  409.6 5.9 %gather_fusion.1 = bf16[40,12,64,128]{3,2,1,0:T(8,128)(2,1)} fusion(bf16[16,12,64,128]{3,2,1,0:T(8,128)(2,1)S(1)} %copy-done, s32[1024]{0:T(1024)S(1)} %pad_clamp_fusion.7), kind=kCustom, calls=%fused_computation.2.clone.1.clone | custom fusion | bytes 15728800 | tf_op jit(solution)/shard_map/while/body/eval_jaxpr/gather | solution.py:72
  415.5 13.3 %reshape.459 = bf16[40,12,8192]{2,1,0:T(8,128)(2,1)} reshape(bf16[40,12,64,128]{3,2,1,0:T(8,128)(2,1)} %gather_fusion.1) | data formatting | bytes 15728640 | tf_op jit(solution)/shard_map/while/body/eval_jaxpr/vmap()/reshape | solution.py:12
  428.8 10.7 %convolution_convert_fusion.4 = bf16[40,12,8192]{2,1,0:T(8,128)(2,1)} fusion(bf16[40,12,8192]{2,1,0:T(8,128)(2,1)} %reshape.459, s32[40,12]{1,0:T(8,128)S(1)} %copy-done.5, s32[12]{0:T(128)S(1)} %copy-done.12), kind=kOutput, calls=%fused_computation.12.clone.1.clone | convolution fusion | flops 98309760 | bytes 15730608 | tf_op jit(solution)/shard_map/while/body/eval_jaxpr/vmap()/dot_general | solution.py:14
  439.5 13.7 %reshape.460 = bf16[40,12,64,128]{3,2,1,0:T(8,128)(2,1)} reshape(bf16[40,12,8192]{2,1,0:T(8,128)(2,1)} %convolution_convert_fusion.4) | data formatting | bytes 15728640 | tf_op jit(solution)/shard_map/while/body/eval_jaxpr/vmap()/reshape | solution.py:16
  453.2 7.1 %convolution_bitcast_fusion.4 = f32[40,64,64]{2,1,0:T(8,128)S(1)} fusion(bf16[40,12,64,128]{3,2,1,0:T(8,128)(2,1)} %reshape.460, bf16[4,12,64,128]{3,2,1,0:T(8,128)(2,1)S(1)} %copy-done.3, s32[]{:T(128)S(6)} %copy.177), kind=kOutput, calls=%fused_computation.13.clone.1.clone | convolution fusion | flops 503316480 | bytes 8716292 | tf_op jit(solution)/shard_map/while/body/eval_jaxpr/vmap(arc,asc->ars)/dot_general | solution.py:18
  462.4 1.7 dynamic_update_slice.6
  468.2 2.5 reshape.458
  470.7 5.9 %gather_fusion.1 = bf16[40,12,64,128]{3,2,1,0:T(8,128)(2,1)} fusion(bf16[16,12,64,128]{3,2,1,0:T(8,128)(2,1)S(1)} %copy-done, s32[1024]{0:T(1024)S(1)} %pad_clamp_fusion.7), kind=kCustom, calls=%fused_computation.2.clone.1.clone | custom fusion | bytes 15728800 | tf_op jit(solution)/shard_map/while/body/eval_jaxpr/gather | solution.py:72
  476.6 13.3 %reshape.459 = bf16[40,12,8192]{2,1,0:T(8,128)(2,1)} reshape(bf16[40,12,64,128]{3,2,1,0:T(8,128)(2,1)} %gather_fusion.1) | data formatting | bytes 15728640 | tf_op jit(solution)/shard_map/while/body/eval_jaxpr/vmap()/reshape | solution.py:12
  489.9 10.7 %convolution_convert_fusion.4 = bf16[40,12,8192]{2,1,0:T(8,128)(2,1)} fusion(bf16[40,12,8192]{2,1,0:T(8,128)(2,1)} %reshape.459, s32[40,12]{1,0:T(8,128)S(1)} %copy-done.5, s32[12]{0:T(128)S(1)} %copy-done.12), kind=kOutput, calls=%fused_computation.12.clone.1.clone | convolution fusion | flops 98309760 | bytes 15730608 | tf_op jit(solution)/shard_map/while/body/eval_jaxpr/vmap()/dot_general | solution.py:14
  500.6 13.7 %reshape.460 = bf16[40,12,64,128]{3,2,1,0:T(8,128)(2,1)} reshape(bf16[40,12,8192]{2,1,0:T(8,128)(2,1)} %convolution_convert_fusion.4) | data formatting | bytes 15728640 | tf_op jit(solution)/shard_map/while/body/eval_jaxpr/vmap()/reshape | solution.py:16
  514.3 7.1 %convolution_bitcast_fusion.4 = f32[40,64,64]{2,1,0:T(8,128)S(1)} fusion(bf16[40,12,64,128]{3,2,1,0:T(8,128)(2,1)} %reshape.460, bf16[4,12,64,128]{3,2,1,0:T(8,128)(2,1)S(1)} %copy-done.3, s32[]{:T(128)S(6)} %copy.177), kind=kOutput, calls=%fused_computation.13.clone.1.clone | convolution fusion | flops 503316480 | bytes 8716292 | tf_op jit(solution)/shard_map/while/body/eval_jaxpr/vmap(arc,asc->ars)/dot_general | solution.py:18
  523.5 1.7 dynamic_update_slice.6
  527.6 1.9 reshape.306
  530.5 3.5 fusion.9
  (158 shorter events, 45.8 us)
Async XLA Ops:
  9.4 16.3 %all-to-all-start = ((s32[32,1,2]{2,1,0:T(1,128)}), s32[32,1,2]{2,1,0:T(1,128)S(1)}, u32[]{:S(2)}, u32[]{:S(2)}) async-start(s32[32,1,2]{2,1,0:T(1,128)} %bitcast.28), calls=%async_computation | async-start | bytes 32768 | tf_op jit(solution)/shard_map/all_to_all | solution.py:93
  19.6 6.3 %copy-start.15 = (pred[4,64]{1,0:T(4,128)(4,1)}, pred[4,64]{1,0:T(4,128)(4,1)S(1)}, u32[]{:S(2)}) copy-start(pred[4,64]{1,0:T(4,128)(4,1)S(1)} %iota_compare_fusion.5) | copy-start | bytes 772
  19.7 0.6 copy-start.9
  22.7 10.4 %copy-start.1 = (bf16[4,12,64,128]{3,2,1,0:T(8,128)(2,1)}, bf16[4,12,64,128]{3,2,1,0:T(8,128)(2,1)S(1)}, u32[]{:S(2)}) copy-start(bf16[4,12,64,128]{3,2,1,0:T(8,128)(2,1)S(1)} %broadcast_select_fusion.2) | copy-start | bytes 2359300
  28.8 21.9 %all-to-all-start.1 = ((bf16[32,2,4096]{2,1,0:T(2,128)(2,1)}), bf16[32,2,4096]{2,1,0:T(2,128)(2,1)S(1)}, u32[]{:S(2)}, u32[]{:S(2)}) async-start(bf16[32,2,4096]{2,1,0:T(2,128)(2,1)} %broadcast_select_fusion.1), calls=%async_computation.1 | async-start | bytes 1048576 | tf_op jit(solution)/shard_map/all_to_all | solution.py:108
  50.6 182.5 %all-to-all-start.2 = ((bf16[32,2,12,64,128]{4,3,2,1,0:T(8,128)(2,1)}), bf16[32,2,12,64,128]{4,3,2,1,0:T(8,128)(2,1)}, u32[]{:S(2)}, u32[]{:S(2)}) async-start(bf16[32,2,12,64,128]{4,3,2,1,0:T(8,128)(2,1)} %broadcast_select_fusion), calls=%async_computation.2 | async-start | bytes 25165824 | tf_op jit(solution)/shard_map/all_to_all | solution.py:107
  58.1 2.4 copy-start.2
  58.1 222.6 %all-gather.3.cloned.1.call-start = ((), (), s32[]{:S(2)}) async-start(), calls=%async_computation.4 | async-start | bytes 3932160 | tf_op jit(solution)/shard_map/all_gather | solution.py:62
  58.8 3.9 copy-start.13
  59.9 14.6 %copy-start.11 = (s32[512,12]{0,1:T(8,128)S(1)}, s32[512,12]{0,1:T(8,128)}, u32[]{:S(2)}) copy-start(s32[512,12]{0,1:T(8,128)} %param.14) | copy-start | bytes 73732
  252.9 274.6 %all-to-all-start.3 = ((f32[32,2,4096]{2,1,0:T(2,128)}), f32[32,2,4096]{2,1,0:T(2,128)}, u32[]{:S(2)}, u32[]{:S(2)}) async-start(f32[32,2,4096]{2,1,0:T(2,128)} %reshape.305), calls=%async_computation.3 | async-start | bytes 2097152 | tf_op jit(solution)/shard_map/all_to_all | solution.py:118
  280.6 6.6 %copy-start = (bf16[16,12,64,128]{3,2,1,0:T(8,128)(2,1)S(1)}, bf16[16,12,64,128]{3,2,1,0:T(8,128)(2,1)}, u32[]{:S(2)}) copy-start(bf16[16,12,64,128]{3,2,1,0:T(8,128)(2,1)} %get-tuple-element.202) | copy-start | bytes 9437188 | tf_op jit(solution)/shard_map/while
  293.2 13.3 %copy-start.5 = (s32[40,12]{1,0:T(8,128)S(1)}, s32[40,12]{1,0:T(8,128)}, u32[]{:S(2)}) copy-start(s32[40,12]{1,0:T(8,128)} %gather_fusion.2) | copy-start | bytes 5764 | tf_op jit(solution)/shard_map/while
  293.2 13.3 %copy-start.12 = (s32[12]{0:T(128)S(1)}, s32[12]{0:T(128)}, u32[]{:S(2)}) copy-start(s32[12]{0:T(128)} %fusion.86) | copy-start | bytes 148 | tf_op jit(solution)/shard_map/while
  317.2 13.7 %copy-start.3 = (bf16[4,12,64,128]{3,2,1,0:T(8,128)(2,1)S(1)}, bf16[4,12,64,128]{3,2,1,0:T(8,128)(2,1)}, u32[]{:S(2)}) copy-start(bf16[4,12,64,128]{3,2,1,0:T(8,128)(2,1)} %get-tuple-element.215) | copy-start | bytes 2359300 | tf_op jit(solution)/shard_map/while
  330.9 7.1 %copy-start.4 = (bf16[40,64,64]{2,1,0:T(8,128)(2,1)S(1)}, bf16[40,64,64]{2,1,0:T(8,128)(2,1)}, u32[]{:S(2)}) copy-start(bf16[40,64,64]{2,1,0:T(8,128)(2,1)} %reshape.458) | copy-start | bytes 983044 | tf_op jit(solution)/shard_map/while
  341.8 6.6 %copy-start = (bf16[16,12,64,128]{3,2,1,0:T(8,128)(2,1)S(1)}, bf16[16,12,64,128]{3,2,1,0:T(8,128)(2,1)}, u32[]{:S(2)}) copy-start(bf16[16,12,64,128]{3,2,1,0:T(8,128)(2,1)} %get-tuple-element.202) | copy-start | bytes 9437188 | tf_op jit(solution)/shard_map/while
  354.3 13.3 %copy-start.5 = (s32[40,12]{1,0:T(8,128)S(1)}, s32[40,12]{1,0:T(8,128)}, u32[]{:S(2)}) copy-start(s32[40,12]{1,0:T(8,128)} %gather_fusion.2) | copy-start | bytes 5764 | tf_op jit(solution)/shard_map/while
  354.3 13.3 %copy-start.12 = (s32[12]{0:T(128)S(1)}, s32[12]{0:T(128)}, u32[]{:S(2)}) copy-start(s32[12]{0:T(128)} %fusion.86) | copy-start | bytes 148 | tf_op jit(solution)/shard_map/while
  378.4 13.7 %copy-start.3 = (bf16[4,12,64,128]{3,2,1,0:T(8,128)(2,1)S(1)}, bf16[4,12,64,128]{3,2,1,0:T(8,128)(2,1)}, u32[]{:S(2)}) copy-start(bf16[4,12,64,128]{3,2,1,0:T(8,128)(2,1)} %get-tuple-element.215) | copy-start | bytes 2359300 | tf_op jit(solution)/shard_map/while
  392.1 7.1 %copy-start.4 = (bf16[40,64,64]{2,1,0:T(8,128)(2,1)S(1)}, bf16[40,64,64]{2,1,0:T(8,128)(2,1)}, u32[]{:S(2)}) copy-start(bf16[40,64,64]{2,1,0:T(8,128)(2,1)} %reshape.458) | copy-start | bytes 983044 | tf_op jit(solution)/shard_map/while
  403.0 6.6 %copy-start = (bf16[16,12,64,128]{3,2,1,0:T(8,128)(2,1)S(1)}, bf16[16,12,64,128]{3,2,1,0:T(8,128)(2,1)}, u32[]{:S(2)}) copy-start(bf16[16,12,64,128]{3,2,1,0:T(8,128)(2,1)} %get-tuple-element.202) | copy-start | bytes 9437188 | tf_op jit(solution)/shard_map/while
  415.5 13.3 %copy-start.5 = (s32[40,12]{1,0:T(8,128)S(1)}, s32[40,12]{1,0:T(8,128)}, u32[]{:S(2)}) copy-start(s32[40,12]{1,0:T(8,128)} %gather_fusion.2) | copy-start | bytes 5764 | tf_op jit(solution)/shard_map/while
  415.5 13.3 %copy-start.12 = (s32[12]{0:T(128)S(1)}, s32[12]{0:T(128)}, u32[]{:S(2)}) copy-start(s32[12]{0:T(128)} %fusion.86) | copy-start | bytes 148 | tf_op jit(solution)/shard_map/while
  439.5 13.7 %copy-start.3 = (bf16[4,12,64,128]{3,2,1,0:T(8,128)(2,1)S(1)}, bf16[4,12,64,128]{3,2,1,0:T(8,128)(2,1)}, u32[]{:S(2)}) copy-start(bf16[4,12,64,128]{3,2,1,0:T(8,128)(2,1)} %get-tuple-element.215) | copy-start | bytes 2359300 | tf_op jit(solution)/shard_map/while
  453.2 7.1 %copy-start.4 = (bf16[40,64,64]{2,1,0:T(8,128)(2,1)S(1)}, bf16[40,64,64]{2,1,0:T(8,128)(2,1)}, u32[]{:S(2)}) copy-start(bf16[40,64,64]{2,1,0:T(8,128)(2,1)} %reshape.458) | copy-start | bytes 983044 | tf_op jit(solution)/shard_map/while
  464.1 6.6 %copy-start = (bf16[16,12,64,128]{3,2,1,0:T(8,128)(2,1)S(1)}, bf16[16,12,64,128]{3,2,1,0:T(8,128)(2,1)}, u32[]{:S(2)}) copy-start(bf16[16,12,64,128]{3,2,1,0:T(8,128)(2,1)} %get-tuple-element.202) | copy-start | bytes 9437188 | tf_op jit(solution)/shard_map/while
  476.6 13.3 %copy-start.5 = (s32[40,12]{1,0:T(8,128)S(1)}, s32[40,12]{1,0:T(8,128)}, u32[]{:S(2)}) copy-start(s32[40,12]{1,0:T(8,128)} %gather_fusion.2) | copy-start | bytes 5764 | tf_op jit(solution)/shard_map/while
  476.6 13.3 %copy-start.12 = (s32[12]{0:T(128)S(1)}, s32[12]{0:T(128)}, u32[]{:S(2)}) copy-start(s32[12]{0:T(128)} %fusion.86) | copy-start | bytes 148 | tf_op jit(solution)/shard_map/while
  500.6 13.7 %copy-start.3 = (bf16[4,12,64,128]{3,2,1,0:T(8,128)(2,1)S(1)}, bf16[4,12,64,128]{3,2,1,0:T(8,128)(2,1)}, u32[]{:S(2)}) copy-start(bf16[4,12,64,128]{3,2,1,0:T(8,128)(2,1)} %get-tuple-element.215) | copy-start | bytes 2359300 | tf_op jit(solution)/shard_map/while
  514.3 7.1 %copy-start.4 = (bf16[40,64,64]{2,1,0:T(8,128)(2,1)S(1)}, bf16[40,64,64]{2,1,0:T(8,128)(2,1)}, u32[]{:S(2)}) copy-start(bf16[40,64,64]{2,1,0:T(8,128)(2,1)} %reshape.458) | copy-start | bytes 983044 | tf_op jit(solution)/shard_map/while
  529.5 0.9 copy-start.6
  529.5 1.0 copy-start.7
  529.5 1.0 copy-start.8
  529.6 0.9 copy-start.10
  529.6 0.9 copy-start.14
  529.6 0.9 copy-start.16
  529.6 0.9 copy-start.17
Sparse Core Ops, SparseCore 0:
  60.5 40.7 all-gather.2
where the time goes:
time: 545 us; the launch traced here: 542 us
  local copies, waits for them, and re-layouts  198 us (36%)
  waiting for transfers between devices  159 us (29%)
  matrix products  91 us (17%)
  starting transfers between devices  48.8 us (9%)
  other arithmetic  19.9 us (4%)
  between operations  13.8 us (3%)
  blocking collectives  10.9 us (2%)
    all_to_all x1, waiting for transfers between devices, on_device(): lax.all_to_all(send_coeff, 'occ', split_axis=0, concat_axis=0, tiled=True)  155 us
    reshape x5, local copies, waits for them, and re-layouts, intersection(): aligned = jnp.dot(matches, flat, preferred_element_type=jnp.float32).asty...  57.8 us
    reshape x5, local copies, waits for them, and re-layouts, intersection(): flat = right_coeff.reshape(right_coeff.shape[0], -1)  55.9 us
    dot_general x5, matrix products, intersection(): jnp.dot(matches, flat, preferred_element_type=jnp.float32)  45 us
    dot_general x5, matrix products, intersection(): jnp.einsum('arc,asc->ars', left_coeff, aligned, preferred_element_type=jn...  30.4 us
    all_to_all x1, starting transfers between devices, on_device(): lax.all_to_all(outgoing.reshape(occ_count, capacity, -1), 'occ', split_ax...  27.7 us
    gather x4, local copies, waits for them, and re-layouts, near_term(): group_coeff[chosen]  23.6 us
  transfers between devices with their start and end apart: 5, of which 2 were waited for; matrix products, arithmetic and copies ran while one was open for 55% of the time, Pallas kernels for 0%

commit v1 on v0

v1 whole, which is shorter than its diff:
```python
import jax
import jax.numpy as jnp
from jax import lax
from jax.sharding import PartitionSpec as P

NPNO = 64
KN = 2
HI = lax.Precision.HIGHEST


def on_device(coeffs, amplitudes, denominators, pno_count, domains, far_owner, far_pair, near_pair):
    n = coeffs.shape[0]
    domb, npno, blk = coeffs.shape[1:]
    n_occ = lax.axis_size("occ")
    n_rep = lax.axis_size("rep")
    nblk = 32
    occ = lax.axis_index("occ")
    rep = lax.axis_index("rep")
    group = n_rep * n
    live = jnp.arange(npno, dtype=jnp.int32)[None, :] < pno_count[:, None]
    live2 = live[:, :, None] & live[:, None, :]
    amp = jnp.where(live2.reshape(n, -1), amplitudes, jnp.zeros((), jnp.bfloat16))
    gc = lax.all_gather(coeffs, "rep", axis=0, tiled=True)
    ga = lax.all_gather(amp, "rep", axis=0, tiled=True)
    gdom = lax.dynamic_slice_in_dim(domains, occ * group, group, 0)

    def dense(c, dom):
        hot = dom[:, None, :] == jnp.arange(nblk, dtype=jnp.int32)[None, :, None]
        slot = jnp.sum(jnp.where(hot, jnp.arange(domb, dtype=jnp.int32)[None, None, :], 0), axis=2)
        have = jnp.any(hot, axis=2)
        g = c[jnp.arange(c.shape[0])[:, None], slot]
        return jnp.where(have[:, :, None, None], g, jnp.zeros((), jnp.bfloat16))

    gd = dense(gc, gdom)
    hd = lax.dynamic_slice_in_dim(gd, rep * n, n, 0)
    counts = jnp.sum((near_pair[:, :, None] == jnp.arange(group)[None, None, :]).astype(jnp.float32), axis=1)
    S = jnp.einsum("pbrc,qbsc->pqrs", hd, gd, preferred_element_type=jnp.float32)
    gt = ga.reshape(group, npno, npno).astype(jnp.float32)
    U = jnp.einsum("pqab,qbc->pqac", S, gt, precision=HI) * counts[:, :, None, None]
    near = jnp.einsum("pqac,pqdc->pad", U, S, precision=HI)

    rid = (far_owner * n + far_pair).reshape(-1)
    req = rid.shape[0]
    per = domb * npno * blk // (n_occ * 8 * blk)
    sl = coeffs.reshape(n, n_occ, per, 8, blk).transpose(1, 0, 2, 3, 4)
    ta = amp.reshape(n, n_occ, -1).transpose(1, 0, 2)
    rq = lax.all_gather(rid, "occ", axis=0, tiled=False)
    r1 = lax.all_to_all(sl, "occ", 0, 0, tiled=True).reshape(n_occ * n, per, 8, blk)
    rt = lax.all_to_all(ta, "occ", 0, 0, tiled=True).reshape(n_occ * n, -1)
    f = lax.all_to_all(r1[rq], "occ", 0, 0, tiled=True)
    ft = lax.all_to_all(rt[rq], "occ", 0, 0, tiled=True)
    fc = f.transpose(1, 0, 2, 3, 4).reshape(req, domb, npno, blk)
    fT = ft.transpose(1, 0, 2).reshape(req, npno, npno).astype(jnp.float32)
    far_ids = (far_owner.reshape(-1) * n_rep + rep) * n + far_pair.reshape(-1)
    fd = dense(fc, domains[far_ids]).reshape(n, KN, nblk, npno, blk)
    SF = jnp.einsum("pbrc,pkbsc->pkrs", hd, fd, preferred_element_type=jnp.float32)
    UF = jnp.einsum("pkab,pkbc->pkac", SF, fT.reshape(n, KN, npno, npno), precision=HI)
    far = jnp.einsum("pkac,pkdc->pad", UF, SF, precision=HI)
    T = amp.reshape(n, npno, npno).astype(jnp.float32)
    V = jnp.einsum("pab,pkbc->pkac", T, SF, precision=HI)
    back = jnp.einsum("pkab,pkac->pkbc", SF, V, precision=HI).reshape(req, n_occ, -1)
    bk = lax.all_to_all(back.transpose(1, 0, 2), "occ", 0, 0, tiled=True).reshape(n_occ * req, -1)
    hot = (jnp.arange(n_occ * n)[:, None] == rq.reshape(-1)[None, :]).astype(jnp.float32)
    bs = jnp.dot(hot, bk, precision=HI).reshape(n_occ, n, -1)
    bb = lax.all_to_all(bs, "occ", 0, 0, tiled=True).transpose(1, 0, 2).reshape(n, npno, npno)
    den = denominators[:, :, None] + denominators[:, None, :]
    out = jnp.where(live2, den * T + near + far + bb, jnp.zeros((), jnp.float32))
    return out.reshape(n, npno * npno)


def solution(mesh):
    in_specs = (
        P(("occ", "rep"), None, None, None),
        P(("occ", "rep"), None),
        P(("occ", "rep"), None),
        P(("occ", "rep")),
        P(),
        P(("occ", "rep"), None),
        P(("occ", "rep"), None),
        P(("occ", "rep"), None),
    )
    return jax.shard_map(
        on_device, mesh=mesh, in_specs=in_specs, out_specs=P(("occ", "rep"), None), check_vma=False
    )
```

time: 545 us -> 160 us (0.29)
  local copies, waits for them, and re-layouts: 198 us -> 28.4 us
  waiting for transfers between devices: 159 us -> 25.1 us
  matrix products: 91 us -> 12.7 us
  blocking collectives: 10.9 us -> 37.6 us
  starting transfers between devices: 48.8 us -> 33.5 us
  other arithmetic: 19.9 us -> 8.26 us
    all_to_all x4 -> x6, waiting for transfers between devices: 158 us -> 24.4 us  [the longest x1 6.97 us: on_device(): lax.all_to_all(bs, 'occ', 0, 0, tiled=True).transpose(1, 0, 2)]
    reshape x22 -> x8, local copies, waits for them, and re-layouts: 129 us -> 4.99 us  [the longest x2 3 us: on_device(): T = amp.reshape(n, npno, npno).astype(jnp.float32)]
    dot_general x24 -> x9, matrix products: 91 us -> 12.7 us  [the longest x1 4.5 us: on_device(): jnp.einsum('pbrc,qbsc->pqrs', hd, gd, preferred_element_type=jnp.float32)]
    gather x21 -> x6, local copies, waits for them, and re-layouts: 53 us -> 17 us  [the longest x2 12.8 us: dense(): g = c[jnp.arange(c.shape[0])[:, None], slot]]
    all_gather x1 -> x2, blocking collectives: 10.9 us -> 37.6 us  [the longest x1 27.1 us: on_device(): rq = lax.all_gather(rid, 'occ', axis=0, tiled=False)]
    all_to_all x4 -> x6, starting transfers between devices: 48.8 us -> 33.5 us  [the longest x1 9.42 us: on_device(): rt = lax.all_to_all(ta, 'occ', 0, 0, tiled=True).reshape(n_occ * n, -1)]
    select_n x10 -> x4, other arithmetic: 17.9 us -> 5.82 us  [the longest x1 4.42 us: dense(): return jnp.where(have[:, :, None, None], g, jnp.zeros((), jnp.bfloat16))]
    dynamic_update_slice x4 -> x0, local copies, waits for them, and re-layouts: 6.79 us -> none  [on_device(): near_gain = lax.map(near_term, (coeff_masked, home_dom, near_pair))]
  transfers between devices with their start and end apart: 5 -> 7, of which waited for: 2 -> 5; matrix products, arithmetic and copies ran while one was open for 55% -> 16% of each run, Pallas kernels for 0% -> 0%
where the time goes in v1:
time: 160 us; the launch traced here: 159 us
  blocking collectives  37.6 us (24%)
  starting transfers between devices  33.5 us (21%)
  local copies, waits for them, and re-layouts  28.4 us (18%)
  waiting for transfers between devices  25.1 us (16%)
  between operations  13.8 us (9%)
  matrix products  12.7 us (8%)
  other arithmetic  8.26 us (5%)
    all_gather x1, blocking collectives, on_device(): rq = lax.all_gather(rid, 'occ', axis=0, tiled=False)  27.1 us
    gather x2, local copies, waits for them, and re-layouts, dense(): g = c[jnp.arange(c.shape[0])[:, None], slot]  12.8 us
    all_gather x1, blocking collectives, on_device(): ga = lax.all_gather(amp, 'rep', axis=0, tiled=True)  10.5 us
    all_to_all x1, starting transfers between devices, on_device(): rt = lax.all_to_all(ta, 'occ', 0, 0, tiled=True).reshape(n_occ * n, -1)  9.42 us
    all_to_all x1, waiting for transfers between devices, on_device(): lax.all_to_all(bs, 'occ', 0, 0, tiled=True).transpose(1, 0, 2)  6.97 us
    all_to_all x1, starting transfers between devices, on_device(): ft = lax.all_to_all(rt[rq], 'occ', 0, 0, tiled=True)  5.76 us
    all_to_all x1, starting transfers between devices, on_device(): lax.all_to_all(back.transpose(1, 0, 2), 'occ', 0, 0, tiled=True)  5.51 us
    all_to_all x1, waiting for transfers between devices, on_device(): ft = lax.all_to_all(rt[rq], 'occ', 0, 0, tiled=True)  5.32 us
  transfers between devices with their start and end apart: 7, of which 5 were waited for; matrix products, arithmetic and copies ran while one was open for 16% of the time, Pallas kernels for 0%

profile of v1, /device:TPU:1, one launch (start us, length us, event | category | flops | bytes accessed | tf_op | source)
XLA Modules:
  0.0 159.3 jit_solution(6889075763457462990)
XLA Ops:
  6.5 0.7 all-gather.4.cloned.1.call-update
  7.3 0.7 iota_compare_fusion.3
  8.0 0.6 copy-done.6
  8.7 0.1 and.22
  8.8 1.4 broadcast_select_fusion.1
  10.2 9.4 %all-to-all-start.2 = ((bf16[32,4,128]{2,1,0:T(4,128)(2,1)}), bf16[32,4,128]{2,1,0:T(4,128)(2,1)S(1)}, u32[]{:S(2)}, u32[]{:S(2)}) async-start(bf16[32,4,128]{2,1,0:T(4,128)(2,1)} %bitcast.28), calls=%async_computation.2 | async-start | bytes 65536 | tf_op jit(solution)/shard_map/all_to_all | solution.py:49
  19.6 2.1 %copy.80 = bf16[32,4,3,8,128]{4,3,2,1,0:T(8,128)(2,1)} copy(bf16[32,4,3,8,128]{4,3,2,0,1:T(8,128)(2,1)} %bitcast.107) | data formatting | bytes 1572864 | tf_op jit(solution)/shard_map/transpose | solution.py:45
  21.7 5.2 %all-to-all-done.2 = bf16[32,4,128]{2,1,0:T(4,128)(2,1)S(1)} async-done(((bf16[32,4,128]{2,1,0:T(4,128)(2,1)}), bf16[32,4,128]{2,1,0:T(4,128)(2,1)S(1)}, u32[]{:S(2)}, u32[]{:S(2)}) %all-to-all-start.2) | async-done | bytes 32800 | tf_op jit(solution)/shard_map/all_to_all | solution.py:49
  26.9 4.0 %all-to-all-start = ((bf16[32,4,3,8,128]{4,3,2,1,0:T(8,128)(2,1)}), bf16[32,4,3,8,128]{4,3,2,1,0:T(8,128)(2,1)S(1)}, u32[]{:S(2)}, u32[]{:S(2)}) async-start(bf16[32,4,3,8,128]{4,3,2,1,0:T(8,128)(2,1)} %copy.80), calls=%async_computation | async-start | bytes 1572864 | tf_op jit(solution)/shard_map/all_to_all | solution.py:48
  31.1 27.1 %all-gather.1 = s32[32,1,8]{2,1,0:T(1,128)S(1)} all-gather(s32[1,1,8]{2,1,0:T(1,128)S(1)} %reshape.239), channel_id=1, replica_groups=mesh['occ'=32,'rep'=4] {'occ'}, dimensions={0}, use_global_device_ids=true | all-gather | bytes 1056 | tf_op jit(solution)/shard_map/all_gather | solution.py:47
  58.2 1.5 gather_fusion.4
  59.7 5.8 %all-to-all-start.3 = ((bf16[32,8,128]{2,1,0:T(8,128)(2,1)}), bf16[32,8,128]{2,1,0:T(8,128)(2,1)S(1)}, u32[]{:S(2)}, u32[]{:S(2)}) async-start(bf16[32,8,128]{2,1,0:T(8,128)(2,1)} %bitcast.30), calls=%async_computation.3 | async-start | bytes 131072 | tf_op jit(solution)/shard_map/all_to_all | solution.py:51
  65.5 2.0 %gather_fusion.2 = bf16[256,3,8,128]{3,2,1,0:T(8,128)(2,1)} fusion(bf16[128,3,8,128]{3,2,1,0:T(8,128)(2,1)S(1)} %bitcast.105, s32[1024]{0:T(1024)S(1)} %pad_clamp_fusion), kind=kCustom, calls=%fused_computation.2 | custom fusion | bytes 3146752 | tf_op jit(solution)/shard_map/gather | solution.py:50
  67.5 5.3 %all-to-all-done.3 = bf16[32,8,128]{2,1,0:T(8,128)(2,1)S(1)} async-done(((bf16[32,8,128]{2,1,0:T(8,128)(2,1)}), bf16[32,8,128]{2,1,0:T(8,128)(2,1)S(1)}, u32[]{:S(2)}, u32[]{:S(2)}) %all-to-all-start.3) | async-done | bytes 65568 | tf_op jit(solution)/shard_map/all_to_all | solution.py:51
  72.8 4.1 %all-to-all-start.1 = ((bf16[32,8,3,8,128]{4,3,2,1,0:T(8,128)(2,1)}), bf16[32,8,3,8,128]{4,3,2,1,0:T(8,128)(2,1)S(1)}, u32[]{:S(2)}, u32[]{:S(2)}) async-start(bf16[32,8,3,8,128]{4,3,2,1,0:T(8,128)(2,1)} %bitcast.19), calls=%async_computation.1 | async-start | bytes 3145728 | tf_op jit(solution)/shard_map/all_to_all | solution.py:50
  77.1 0.1 copy.78
  77.2 1.5 reshape.251
  78.8 1.5 reshape.184
  80.6 0.6 gather_fusion.1
  81.5 0.6 broadcast_in_dim.101
  82.1 0.5 broadcast.203
  82.6 0.6 reduce.3
  83.2 0.7 eq.78
  83.9 10.5 %all-gather = bf16[4,4,4096]{2,1,0:T(4,128)(2,1)S(1)} all-gather(bf16[1,4,4096]{2,1,0:T(4,128)(2,1)} %bitcast), channel_id=1, replica_groups=mesh['occ'=32,'rep'=4] {'rep'}, dimensions={0}, use_global_device_ids=true | all-gather | bytes 163840 | tf_op jit(solution)/shard_map/all_gather | solution.py:24
  94.4 0.3 reshape.185
  94.7 0.6 convert_reduce_fusion
  95.5 0.1 reshape.191
  95.6 4.2 %all-to-all-done.1 = bf16[32,8,3,8,128]{4,3,2,1,0:T(8,128)(2,1)S(1)} async-done(((bf16[32,8,3,8,128]{4,3,2,1,0:T(8,128)(2,1)}), bf16[32,8,3,8,128]{4,3,2,1,0:T(8,128)(2,1)S(1)}, u32[]{:S(2)}, u32[]{:S(2)}) %all-to-all-start.1) | async-done | bytes 1572896 | tf_op jit(solution)/shard_map/all_to_all | solution.py:50
  99.8 0.3 copy.82
  100.0 3.3 %gather_fusion.3 = bf16[256,64,128]{2,1,0:T(8,128)(2,1)} fusion(bf16[8,12,64,128]{3,2,1,0:T(8,128)(2,1)S(1)} %bitcast.103, s32[256]{0:T(256)S(1)} %reshape.218), kind=kCustom, calls=%fused_computation.3 | custom fusion | bytes 8390656 | tf_op jit(solution)/shard_map/gather | solution.py:31
  103.4 9.5 %gather_fusion = bf16[512,64,128]{2,1,0:T(8,128)(2,1)} fusion(bf16[16,12,64,128]{3,2,1,0:T(8,128)(2,1)} %all-gather.4.cloned.1.call-done, s32[512]{0:T(512)S(1)} %reshape.196), kind=kCustom, calls=%fused_computation | custom fusion | bytes 16781312 | tf_op jit(solution)/shard_map/gather | solution.py:31
  112.9 4.4 %broadcast_select_fusion = bf16[16,32,64,128]{3,2,1,0:T(8,128)(2,1)S(1)} fusion(bf16[16,32,64,128]{3,2,1,0:T(8,128)(2,1)} %bitcast.102, pred[16,32]{1,0:T(8,128)(4,1)S(1)} %fusion.40), kind=kLoop, calls=%fused_computation.7 | loop fusion | flops 4194304 | bytes 16777728 | tf_op jit(solution)/shard_map/jit(_where)/select_n | solution.py:32
  117.3 4.5 %fusion.14 = f32[4,16,64,64]{2,3,0,1:T(8,128)S(1)} fusion(bf16[16,32,64,128]{3,2,1,0:T(8,128)(2,1)S(1)} %broadcast_select_fusion, s32[]{:T(128)S(6)} %select_n.72), kind=kOutput, calls=%fused_computation.21 | convolution fusion | flops 2147483648 | bytes 11534340 | tf_op jit(solution)/shard_map/pbrc,qbsc->pqrs/dot_general | solution.py:37
  121.9 1.6 fusion.2
  123.4 0.3 fusion.29
  123.7 0.5 fusion.32
  124.4 0.7 copy.115
  125.1 5.5 %all-to-all-start.4 = ((f32[32,8,128]{2,1,0:T(8,128)}), f32[32,8,128]{2,1,0:T(8,128)S(1)}, u32[]{:S(2)}, u32[]{:S(2)}) async-start(f32[32,8,128]{2,1,0:T(8,128)} %bitcast.101), calls=%async_computation.4 | async-start | bytes 262144 | tf_op jit(solution)/shard_map/all_to_all | solution.py:62
  130.6 1.2 fusion.10
  131.9 3.7 %fusion.25 = f32[4,64,64]{2,1,0:T(8,128)S(1)} fusion(f32[4,16,64,64]{2,3,0,1:T(8,128)S(1)} %fusion.14, f32[16,64,4,64]{3,1,0,2:T(8,128)S(1)} %fusion.10, f32[4,16]{1,0:T(4,128)S(1)} %copy-done.5, bf16[4,64,64]{2,1,0:T(8,128)(2,1)S(1)} %copy-done.1, f32[4,64]{1,0:T(4,128)S(1)} %copy-done.4), kind=kOutput, calls=%fused_computation.27 | convolution fusion | flops 201654272 | bytes 2196736 | tf_op jit(solution)/shard_map/pqac,pqdc->pad/dot_general | solution.py:40
  135.5 2.7 %all-to-all-done.4 = f32[32,8,128]{2,1,0:T(8,128)S(1)} async-done(((f32[32,8,128]{2,1,0:T(8,128)}), f32[32,8,128]{2,1,0:T(8,128)S(1)}, u32[]{:S(2)}, u32[]{:S(2)}) %all-to-all-start.4) | async-done | bytes 131104 | tf_op jit(solution)/shard_map/all_to_all | solution.py:62
  138.3 0.3 fusion.37
  138.5 0.7 copy.88
  139.2 4.7 %all-to-all-start.5 = ((f32[32,4,128]{2,1,0:T(4,128)}), f32[32,4,128]{2,1,0:T(4,128)S(1)}, u32[]{:S(2)}, u32[]{:S(2)}) async-start(f32[32,4,128]{2,1,0:T(4,128)} %copy.88), calls=%async_computation.5 | async-start | bytes 131072 | tf_op jit(solution)/shard_map/all_to_all | solution.py:65
  143.9 0.4 fusion.34
  144.3 7.0 %all-to-all-done.5 = f32[32,4,128]{2,1,0:T(4,128)S(1)} async-done(((f32[32,4,128]{2,1,0:T(4,128)}), f32[32,4,128]{2,1,0:T(4,128)S(1)}, u32[]{:S(2)}, u32[]{:S(2)}) %all-to-all-start.5) | async-done | bytes 65568 | tf_op jit(solution)/shard_map/all_to_all | solution.py:65
  151.4 0.4 fusion.24
  151.8 0.7 reshape.195
  (54 shorter events, 1.5 us)
Async XLA Ops:
  6.5 24.3 %copy-start.12 = (s32[4,2]{0,1:T(2,128)S(1)}, s32[4,2]{0,1:T(2,128)}, u32[]{:S(2)}) copy-start(s32[4,2]{0,1:T(2,128)} %param.13) | copy-start | bytes 100
  6.5 24.3 %copy-start.11 = (s32[4,2]{0,1:T(2,128)S(1)}, s32[4,2]{0,1:T(2,128)}, u32[]{:S(2)}) copy-start(s32[4,2]{0,1:T(2,128)} %param.14) | copy-start | bytes 100
  6.5 96.9 %all-gather.4.cloned.1.call-start = ((), (), s32[]{:S(2)}) async-start(), calls=%async_computation.6 | async-start | bytes 3932160 | tf_op jit(solution)/shard_map/all_gather | solution.py:23
  8.0 0.6 copy-start.6
  10.2 16.7 %all-to-all-start.2 = ((bf16[32,4,128]{2,1,0:T(4,128)(2,1)}), bf16[32,4,128]{2,1,0:T(4,128)(2,1)S(1)}, u32[]{:S(2)}, u32[]{:S(2)}) async-start(bf16[32,4,128]{2,1,0:T(4,128)(2,1)} %bitcast.28), calls=%async_computation.2 | async-start | bytes 65536 | tf_op jit(solution)/shard_map/all_to_all | solution.py:49
  26.9 32.8 %all-to-all-start = ((bf16[32,4,3,8,128]{4,3,2,1,0:T(8,128)(2,1)}), bf16[32,4,3,8,128]{4,3,2,1,0:T(8,128)(2,1)S(1)}, u32[]{:S(2)}, u32[]{:S(2)}) async-start(bf16[32,4,3,8,128]{4,3,2,1,0:T(8,128)(2,1)} %copy.80), calls=%async_computation | async-start | bytes 1572864 | tf_op jit(solution)/shard_map/all_to_all | solution.py:48
  59.7 13.1 %all-to-all-start.3 = ((bf16[32,8,128]{2,1,0:T(8,128)(2,1)}), bf16[32,8,128]{2,1,0:T(8,128)(2,1)S(1)}, u32[]{:S(2)}, u32[]{:S(2)}) async-start(bf16[32,8,128]{2,1,0:T(8,128)(2,1)} %bitcast.30), calls=%async_computation.3 | async-start | bytes 131072 | tf_op jit(solution)/shard_map/all_to_all | solution.py:51
  67.5 9.5 %copy-start.3 = (s32[512,12]{0,1:T(8,128)S(1)}, s32[512,12]{0,1:T(8,128)}, u32[]{:S(2)}) copy-start(s32[512,12]{0,1:T(8,128)} %param.12) | copy-start | bytes 73732
  72.8 21.9 %copy-start.10 = (s32[4,40]{1,0:T(4,128)S(1)}, s32[4,40]{1,0:T(4,128)}, u32[]{:S(2)}) copy-start(s32[4,40]{1,0:T(4,128)} %param.15) | copy-start | bytes 1924
  72.8 26.9 %all-to-all-start.1 = ((bf16[32,8,3,8,128]{4,3,2,1,0:T(8,128)(2,1)}), bf16[32,8,3,8,128]{4,3,2,1,0:T(8,128)(2,1)S(1)}, u32[]{:S(2)}, u32[]{:S(2)}) async-start(bf16[32,8,3,8,128]{4,3,2,1,0:T(8,128)(2,1)} %bitcast.19), calls=%async_computation.1 | async-start | bytes 3145728 | tf_op jit(solution)/shard_map/all_to_all | solution.py:50
  117.3 4.5 %copy-start = (bf16[256,64,128]{2,1,0:T(8,128)(2,1)S(1)}, bf16[256,64,128]{2,1,0:T(8,128)(2,1)}, u32[]{:S(2)}) copy-start(bf16[256,64,128]{2,1,0:T(8,128)(2,1)} %gather_fusion.3) | copy-start | bytes 12582916
  117.3 4.5 %copy-start.9 = (pred[4,2,32]{2,1,0:T(4,128)(4,1)S(1)}, pred[4,2,32]{2,1,0:T(4,128)(4,1)}, u32[]{:S(2)}) copy-start(pred[4,2,32]{2,1,0:T(4,128)(4,1)} %broadcast_in_dim.101) | copy-start | bytes 772
  121.9 1.6 copy-start.2
  125.1 13.2 %all-to-all-start.4 = ((f32[32,8,128]{2,1,0:T(8,128)}), f32[32,8,128]{2,1,0:T(8,128)S(1)}, u32[]{:S(2)}, u32[]{:S(2)}) async-start(f32[32,8,128]{2,1,0:T(8,128)} %bitcast.101), calls=%async_computation.4 | async-start | bytes 262144 | tf_op jit(solution)/shard_map/all_to_all | solution.py:62
  130.6 1.2 copy-start.1
  130.6 1.2 copy-start.4
  130.6 1.2 copy-start.5
  131.8 6.4 %copy-start.8 = (s32[256]{0:T(256)S(1)}, s32[256]{0:T(256)}, u32[]{:S(2)}) copy-start(s32[256]{0:T(256)} %eq.78) | copy-start | bytes 3076
  131.8 19.5 %copy-start.7 = (pred[4,64]{1,0:T(4,128)(4,1)S(1)}, pred[4,64]{1,0:T(4,128)(4,1)}, u32[]{:S(2)}) copy-start(pred[4,64]{1,0:T(4,128)(4,1)} %copy-done.6) | copy-start | bytes 772
  139.2 12.0 %all-to-all-start.5 = ((f32[32,4,128]{2,1,0:T(4,128)}), f32[32,4,128]{2,1,0:T(4,128)S(1)}, u32[]{:S(2)}, u32[]{:S(2)}) async-start(f32[32,4,128]{2,1,0:T(4,128)} %copy.88), calls=%async_computation.5 | async-start | bytes 131072 | tf_op jit(solution)/shard_map/all_to_all | solution.py:65
Sparse Core Ops, SparseCore 0:
  9.0 42.5 all-gather.3

commit v2 on v1

v2 whole, which is shorter than its diff:
```python
import jax
import jax.numpy as jnp
from jax import lax
from jax.experimental import pallas as pl
from jax.experimental.pallas import tpu as pltpu
from jax.sharding import PartitionSpec as P

MESH = pl.DeviceIdType.MESH
NBLK = 32
KN = 2
BF = jnp.bfloat16
F32 = jnp.float32
NT = (((1,), (1,)), ((), ()))


def split(x):
    hi = x.astype(BF)
    return hi, (x - hi.astype(F32)).astype(BF)


def mm(a, b):
    return jnp.dot(a, b, preferred_element_type=F32)


def mm_nt(a, b):
    return lax.dot_general(a, b, NT, preferred_element_type=F32)


def kernel(
    n_occ, n_rep, n, domb, npno, blk,
    cnt, rids, snear, sfar, counts, coef, coefs, amp, den, ridrow,
    out,
    G, F, R1, SF, GT, RT, ST, FT, RQ, rqs, acc, SH, SL, UH, UL, BD, W, BKs, BKr, BS, BB, X,
    ysend, yrecv, tsend, trecv, p1s, p1r, p2s, p2r, bs, br, lsem,
):
    me = lax.axis_index("occ")
    rep = lax.axis_index("rep")
    right = lax.rem(rep + 1, n_rep)
    left = lax.rem(rep + n_rep - 1, n_rep)
    far2 = lax.rem(rep + 2, n_rep)
    req = n * KN
    group = n * n_rep
    per = domb * npno // 8 // n_occ
    half = n // 2
    lane = lax.broadcasted_iota(jnp.int32, (8, 128), 1)
    sub = lax.broadcasted_iota(jnp.int32, (8, 128), 0)
    low = lane < npno

    def occ_dev(d):
        return {"occ": d}

    def rep_dev(d):
        return {"rep": d}

    barrier = pltpu.get_barrier_semaphore()

    def greet(k, c):
        pl.semaphore_signal(barrier, inc=1, device_id=occ_dev(lax.rem(me + k, n_occ)), device_id_type=MESH)
        return c

    lax.fori_loop(1, n_occ, greet, 0)
    for d in (left, right):
        pl.semaphore_signal(barrier, inc=1, device_id=rep_dev(d), device_id_type=MESH)

    own = pltpu.make_async_copy(
        coef, G.at[pl.ds(rep * n, n), pl.ds(0, domb)], lsem.at[0])
    own.start()
    own1 = pltpu.make_async_copy(
        coefs.at[:, pl.ds(me * per, per)], R1.at[pl.ds(me * n, n)], lsem.at[1])
    own1.start()

    cntv = jnp.zeros((8, 128), jnp.int32)
    for p in range(n):
        cntv = jnp.where(sub == p, cnt[p], cntv)
    col = lax.rem(lane, npno)
    up = lane // npno
    for i in range(npno * npno // 128):
        x = amp[:, 128 * i : 128 * i + 128].astype(F32)
        x = jnp.concatenate([x, jnp.zeros((8 - n, 128), F32)], axis=0)
        live = (2 * i + up < cntv) & (col < cntv)
        GT[rep, pl.ds(8 * i, 8), :] = jnp.where(live, x, 0.0)
    G[:, domb] = jnp.zeros((group, npno, blk), BF)
    F[:, pl.ds(domb * 8, 8)] = jnp.zeros((req, 8, 8, blk), BF)
    RQ[me] = ridrow[...]
    RT[pl.ds(8 * me, 8), :] = GT[rep, pl.ds(8 * me, 8), :]

    pl.semaphore_wait(barrier, n_occ - 1 + 2)

    def plane(k, c):
        d = lax.rem(me + k, n_occ)
        pltpu.make_async_remote_copy(
            ridrow, RQ.at[me], p1s.at[0], p1r.at[0], device_id=occ_dev(d), device_id_type=MESH).start()
        pltpu.make_async_remote_copy(
            GT.at[rep, pl.ds(8 * d, 8)], RT.at[pl.ds(8 * me, 8)], p1s.at[1], p1r.at[1],
            device_id=occ_dev(d), device_id_type=MESH).start()
        pltpu.make_async_remote_copy(
            coefs.at[:, pl.ds(d * per, per)], R1.at[pl.ds(me * n, n)], p1s.at[2], p1r.at[2],
            device_id=occ_dev(d), device_id_type=MESH).start()
        return c

    lax.fori_loop(1, n_occ, plane, 0)

    full = pl.ds(0, domb)

    def ycopy(src, first, dev, s):
        return pltpu.make_async_remote_copy(
            src, G.at[pl.ds(first, half), full], ysend.at[s], yrecv.at[s],
            device_id=rep_dev(dev), device_id_type=MESH)

    sends = []
    s_ra = ycopy(coef.at[pl.ds(0, half)], rep * n, right, 0)
    s_lb = ycopy(coef.at[pl.ds(half, half)], rep * n + half, left, 1)
    s_rb = ycopy(coef.at[pl.ds(half, half)], rep * n + half, right, 2)
    s_la = ycopy(coef.at[pl.ds(0, half)], rep * n, left, 3)
    t_r = pltpu.make_async_remote_copy(
        GT.at[rep], GT.at[rep], tsend.at[0], trecv.at[0], device_id=rep_dev(right), device_id_type=MESH)
    t_l = pltpu.make_async_remote_copy(
        GT.at[rep], GT.at[rep], tsend.at[1], trecv.at[1], device_id=rep_dev(left), device_id_type=MESH)
    for s in (s_ra, s_lb, t_r, t_l, s_rb, s_la):
        s.start()
    sends += [s_ra, s_lb, s_rb, s_la, t_r, t_l]

    def wait_all(ref, sem):
        pltpu.make_async_copy(ref, ref, sem).wait()

    wait_all(RQ.at[pl.ds(0, n_occ - 1)], p1r.at[0])
    table = pltpu.make_async_copy(RQ, rqs, lsem.at[2])
    table.start()
    wait_all(RT.at[pl.ds(0, 8 * (n_occ - 1))], p1r.at[1])
    wait_all(R1.at[pl.ds(0, n * (n_occ - 1))], p1r.at[2])
    own1.wait()
    table.wait()

    def pick(d, j):
        r = rqs[d, 0, lax.rem(d * req + j, 128)]
        return r, r - (r >> 3) * (8 - n)

    for j in range(req):
        r8, r4 = pick(me, j)
        F[j, pl.ds(me * per, per)] = R1[r4]
        FT[pl.ds(8 * me + j, 1), :] = RT[pl.ds(r8, 1), :]

    def gather(d):
        for j in range(req):
            r8, r4 = pick(d, j)
            SF[d, j] = R1[r4]
            ST[pl.ds(8 * d + j, 1), :] = RT[pl.ds(r8, 1), :]

    def ship(d):
        pltpu.make_async_remote_copy(
            SF.at[d], F.at[:, pl.ds(me * per, per)], p2s.at[0], p2r.at[0],
            device_id=occ_dev(d), device_id_type=MESH).start()
        pltpu.make_async_remote_copy(
            ST.at[pl.ds(8 * d, 8)], FT.at[pl.ds(8 * me, 8)], p2s.at[1], p2r.at[1],
            device_id=occ_dev(d), device_id_type=MESH).start()

    gather(lax.rem(me + 1, n_occ))

    def answer(k, c):
        gather(lax.rem(me + k, n_occ))
        ship(lax.rem(me + k - 1, n_occ))
        return c

    lax.fori_loop(2, n_occ, answer, 0)
    ship(lax.rem(me + n_occ - 1, n_occ))

    s_ra.wait_recv()
    f_r = ycopy(G.at[pl.ds(left * n, half), full], left * n, right, 4)
    f_r.start()
    s_lb.wait_recv()
    f_l = ycopy(G.at[pl.ds(right * n + half, half), full], right * n + half, left, 5)
    f_l.start()
    t_r.wait_recv()
    t_l.wait_recv()
    ft = pltpu.make_async_remote_copy(
        GT.at[left], GT.at[left], tsend.at[2], trecv.at[2], device_id=rep_dev(right), device_id_type=MESH)
    ft.start()
    sends += [f_r, f_l, ft]
    s_rb.wait_recv()
    s_la.wait_recv()
    own.wait()
    ft.wait_recv()
    f_r.wait_recv()
    f_l.wait_recv()

    acc[...] = jnp.zeros_like(acc)

    def overlap(b, c):
        hs, gs = [], []
        for t in range(2):
            bb = 2 * b + t
            hs.append(jnp.concatenate(
                [G[rep * n + p, snear[(rep * n + p) * NBLK + bb]] for p in range(n)], axis=0))
            gs.append(jnp.concatenate([G[q, snear[q * NBLK + bb]] for q in range(group)], axis=0))
        acc[...] += mm_nt(jnp.concatenate(hs, axis=1), jnp.concatenate(gs, axis=1))
        return c

    lax.fori_loop(0, NBLK // 2, overlap, 0)

    lane32 = lax.broadcasted_iota(jnp.int32, (npno // 2, 128), 1) < npno

    def place(x, slot, odd):
        other = pltpu.roll(x, npno, 1)
        if odd:
            BD[slot, pl.ds(npno, npno // 2, stride=2), :] = jnp.where(lane32, 0.0, other)
            BD[slot, pl.ds(npno + 1, npno // 2, stride=2), :] = jnp.where(lane32, 0.0, x)
        else:
            BD[slot, pl.ds(0, npno // 2, stride=2), :] = jnp.where(lane32, x, 0.0)
            BD[slot, pl.ds(1, npno // 2, stride=2), :] = jnp.where(lane32, other, 0.0)

    for q in range(group):
        place(GT[q // n, pl.ds(q % n, npno // 2, stride=8), :], q // 2, q % 2)

    low64 = lax.broadcasted_iota(jnp.int32, (npno, 128), 1) < npno

    def project(k, c):
        sl = pl.ds(pl.multiple_of(k * 128, 128), 128)
        hi, lo = split(acc[:, sl])
        SH[:, sl] = hi
        SL[:, sl] = lo
        bd = BD[k].astype(BF)
        u = mm(jnp.concatenate([hi, lo], axis=1), jnp.concatenate([bd, bd], axis=0))
        for p in range(n):
            w = jnp.where(low64, counts[p * group + 2 * k], counts[p * group + 2 * k + 1])
            uh, ul = split(u[p * npno : (p + 1) * npno] * w)
            UH[pl.ds(p * npno, npno), sl] = uh
            UL[pl.ds(p * npno, npno), sl] = ul
        return c

    lax.fori_loop(0, group // 2, project, 0)

    def flat(slot):
        e = W[slot, pl.ds(0, npno // 2, stride=2), :]
        o = W[slot, pl.ds(1, npno // 2, stride=2), :]
        return jnp.where(lane32, e, pltpu.roll(o, npno, 1))

    for p in range(n):
        rows = pl.ds(p * npno, npno)
        g = mm_nt(UH[rows, :], SH[rows, :]) + mm_nt(UL[rows, :], SH[rows, :]) + mm_nt(UH[rows, :], SL[rows, :])
        W[2 * req + p, :, pl.ds(0, npno)] = g

    wait_all(FT.at[pl.ds(0, 8 * (n_occ - 1))], p2r.at[1])
    for j in range(req):
        place(FT[pl.ds(j, npno // 2, stride=8), :], group // 2 + j // 2, j % 2)
    wait_all(F.at[:, pl.ds(0, (n_occ - 1) * per)], p2r.at[0])
    for p in range(n):
        h = jnp.concatenate([G[rep * n + p, a] for a in range(domb)], axis=1)
        f = jnp.concatenate([
            jnp.concatenate([F[KN * p + t, pl.ds(8 * sfar[(KN * p + t) * domb + a], 8)].reshape(npno, blk) for a in range(domb)], axis=1)
            for t in range(KN)], axis=0)
        s = mm_nt(h, f)
        sh, sl_ = split(s)
        bd = BD[group // 2 + p].astype(BF)
        u = mm(jnp.concatenate([sh, sl_], axis=1), jnp.concatenate([bd, bd], axis=0))
        uh, ul = split(u)
        W[2 * req + p, :, pl.ds(0, npno)] += mm_nt(uh, sh) + mm_nt(ul, sh) + mm_nt(uh, sl_)
        odd = p % 2
        tp = BD[rep * (n // 2) + p // 2, pl.ds(odd * npno, npno), :].astype(BF)
        if odd:
            z = jnp.zeros((npno, 128), BF)
            v = mm(tp, jnp.concatenate([z[:npno], sh], axis=0)) + mm(tp, jnp.concatenate([z[:npno], sl_], axis=0))
        else:
            z = jnp.zeros((npno, 128), BF)
            v = mm(tp, jnp.concatenate([sh, z[:npno]], axis=0)) + mm(tp, jnp.concatenate([sl_, z[:npno]], axis=0))
        st = s.T
        th, tl = split(st)
        vh, vl = split(v)
        b = mm(th, vh) + mm(tl, vh) + mm(th, vl)
        W[KN * p, :, :] = b[:npno]
        W[KN * p + 1, :, :] = pltpu.roll(b[npno:], npno, 1)
    for j in range(req):
        BKs[pl.ds(j, npno // 2, stride=8), :] = flat(j)
    for p in range(n):
        X[pl.ds(p, npno // 2, stride=8), :] = flat(2 * req + p)

    def back(src, dst, s):
        def go(k, c):
            d = lax.rem(me + k, n_occ)
            pltpu.make_async_remote_copy(
                src.at[pl.ds(8 * d, 8)], dst.at[pl.ds(8 * me, 8)], bs.at[s], br.at[s],
                device_id=occ_dev(d), device_id_type=MESH).start()
            return c

        lax.fori_loop(1, n_occ, go, 0)
        dst[pl.ds(8 * me, 8), :] = src[pl.ds(8 * me, 8), :]

    rows_in = pl.ds(0, 8 * (n_occ - 1))
    back(BKs, BKr, 0)
    hn = n_occ // 2
    ids = jnp.concatenate(
        [jnp.sum(RQ[pl.ds(h * hn, hn)], axis=0) for h in range(2)], axis=1)
    hot = (lax.broadcasted_iota(jnp.int32, (8 * n_occ, req * n_occ), 0) == ids).astype(F32).astype(BF)
    wait_all(BKr.at[rows_in], br.at[0])
    kh, kl = split(BKr[...])
    BS[...] = mm(hot, kh) + mm(hot, kl)
    back(BS, BB, 1)
    dd = jnp.concatenate([den[...], jnp.zeros((8 - n, npno), F32)], axis=0)
    db = jnp.concatenate([dd, dd], axis=1)
    wait_all(BB.at[rows_in], br.at[1])
    for i in range(npno * npno // 128):
        r = pl.ds(8 * i, 8)
        da = jnp.where(low, dd[:, 2 * i : 2 * i + 1], dd[:, 2 * i + 1 : 2 * i + 2])
        live = (2 * i + up < cntv) & (col < cntv)
        x = (da + db) * GT[rep, r, :] + X[r, :] + BB[r, :]
        out[:, 128 * i : 128 * i + 128] = jnp.where(live, x, 0.0)[:n]

    for s in sends:
        s.wait_send()
    wait_all(RQ.at[pl.ds(0, n_occ - 1)], p1s.at[0])
    wait_all(RT.at[rows_in], p1s.at[1])
    wait_all(R1.at[pl.ds(0, n * (n_occ - 1))], p1s.at[2])
    wait_all(F.at[:, pl.ds(0, (n_occ - 1) * per)], p2s.at[0])
    wait_all(FT.at[rows_in], p2s.at[1])
    wait_all(BKr.at[rows_in], bs.at[0])
    wait_all(BB.at[rows_in], bs.at[1])


def on_device(n_occ, n_rep, coeffs, amplitudes, denominators, pno_count, domains, far_owner, far_pair, near_pair):
    n, domb, npno, blk = coeffs.shape
    occ = lax.axis_index("occ")
    rep = lax.axis_index("rep")
    group = n * n_rep
    req = n * KN
    i32 = jnp.int32
    gdom = lax.dynamic_slice_in_dim(domains, occ * group, group, 0)
    a_id = jnp.arange(domb, dtype=i32) - domb
    hot = gdom[:, None, :] == jnp.arange(NBLK, dtype=i32)[None, :, None]
    snear = (domb + jnp.sum(jnp.where(hot, a_id, 0), axis=2)).reshape(-1)
    far_ids = ((far_owner * n_rep + rep) * n + far_pair).reshape(-1)
    fdom = domains[far_ids]
    hdom = jnp.repeat(lax.dynamic_slice_in_dim(domains, (occ * n_rep + rep) * n, n, 0), KN, axis=0)
    sfar = (domb + jnp.sum(jnp.where(hdom[:, :, None] == fdom[:, None, :], a_id, 0), axis=2)).reshape(-1)
    counts = jnp.sum((near_pair[:, None, :] == jnp.arange(group, dtype=i32)[None, :, None]).astype(F32), axis=2)
    rids = (far_owner * 8 + far_pair).reshape(-1)
    lanes = jnp.arange(128, dtype=i32)
    ridrow = jnp.where(lanes // req == lax.rem(occ, 128 // req), jnp.tile(rids, 128 // req), 0)[None, :]

    smem = pl.BlockSpec(memory_space=pltpu.SMEM)
    vmem = pl.BlockSpec(memory_space=pltpu.VMEM)
    anym = pl.BlockSpec(memory_space=pl.ANY)
    rows = 8 * n_occ
    per = domb * npno // 8 // n_occ
    V = pltpu.VMEM
    dma = pltpu.SemaphoreType.DMA
    import functools
    return pl.pallas_call(
        functools.partial(kernel, n_occ, n_rep, n, domb, npno, blk),
        out_shape=jax.ShapeDtypeStruct((n, npno * npno), F32),
        in_specs=[smem] * 5 + [anym, anym, vmem, vmem, vmem],
        out_specs=vmem,
        scratch_shapes=[
            V((group, domb + 1, npno, blk), BF),
            V((req, (domb + 1) * 8, 8, blk), BF),
            V((n_occ * n, per, 8, blk), BF),
            V((n_occ, req, per, 8, blk), BF),
            V((n_rep, rows, 128), F32),
            V((rows, 128), F32),
            V((rows, 128), F32),
            V((rows, 128), F32),
            V((n_occ, 1, 128), i32),
            pltpu.SMEM((n_occ, 1, 128), i32),
            V((n * npno, group * npno), F32),
            V((n * npno, group * npno), BF),
            V((n * npno, group * npno), BF),
            V((n * npno, group * npno), BF),
            V((n * npno, group * npno), BF),
            V((group // 2 + n, 128, 128), F32),
            V((2 * req + n, npno, 128), F32),
            V((rows, 128), F32),
            V((rows, 128), F32),
            V((rows, 128), F32),
            V((rows, 128), F32),
            V((rows, 128), F32),
            dma((6,)), dma((6,)), dma((3,)), dma((3,)),
            dma((3,)), dma((3,)), dma((2,)), dma((2,)), dma((2,)), dma((2,)), dma((3,)),
        ],
        compiler_params=pltpu.CompilerParams(
            collective_id=0, has_side_effects=True, vmem_limit_bytes=56 * 1024 * 1024),
    )(pno_count, rids, snear, sfar, counts.reshape(-1), coeffs, coeffs.reshape(n, domb * npno // 8, 8, blk),
      amplitudes, denominators, ridrow)


def solution(mesh):
    import functools
    both = ("occ", "rep")
    in_specs = (
        P(both, None, None, None), P(both, None), P(both, None), P(both),
        P(), P(both, None), P(both, None), P(both, None),
    )
    return jax.shard_map(
        functools.partial(on_device, mesh.shape["occ"], mesh.shape["rep"]),
        mesh=mesh, in_specs=in_specs, out_specs=P(both, None), check_vma=False,
    )
```

time: 160 us -> 75.5 us (0.47)
  Pallas kernels: 0 us -> 68.3 us
  blocking collectives: 37.6 us -> 0 us
  starting transfers between devices: 33.5 us -> 0 us
  waiting for transfers between devices: 25.1 us -> 0 us
  local copies, waits for them, and re-layouts: 28.4 us -> 4.98 us
  between operations: 13.8 us -> 0.07 us
  matrix products: 12.7 us -> 0 us
  other arithmetic: 8.26 us -> 1.88 us
    pallas_call x0 -> x1, Pallas kernels: none -> 68.3 us  [on_device(): pl.pallas_call(functools.partial(kernel, n_occ, n_rep, n, domb, npno, blk...]
    all_gather x2 -> x0, blocking collectives: 37.6 us -> none  [the longest x1 27.1 us: on_device(): rq = lax.all_gather(rid, 'occ', axis=0, tiled=False)]
    all_to_all x6 -> x0, starting transfers between devices: 33.5 us -> none  [the longest x1 9.42 us: on_device(): rt = lax.all_to_all(ta, 'occ', 0, 0, tiled=True).reshape(n_occ * n, -1)]
    all_to_all x6 -> x0, waiting for transfers between devices: 24.4 us -> none  [the longest x1 6.97 us: on_device(): lax.all_to_all(bs, 'occ', 0, 0, tiled=True).transpose(1, 0, 2)]
    gather x6 -> x1, local copies, waits for them, and re-layouts: 17 us -> 0.56 us  [on_device(): fdom = domains[far_ids]]
    dot_general x9 -> x0, matrix products: 12.7 us -> none  [the longest x1 4.5 us: on_device(): jnp.einsum('pbrc,qbsc->pqrs', hd, gd, preferred_element_type=jnp.float32)]
    select_n x4 -> x2, other arithmetic: 5.82 us -> 0.61 us  [the longest x1 0.6 us: on_device(): jnp.where(lanes // req == lax.rem(occ, 128 // req), jnp.tile(rids, 128 //...]
    reshape x8 -> x3, local copies, waits for them, and re-layouts: 4.99 us -> 0.76 us  [the longest x1 0.59 us: on_device(): counts.reshape(-1)]
  transfers between devices with their start and end apart: 7 -> 0, of which waited for: 5 -> 0; matrix products, arithmetic and copies ran while one was open for 16% -> 0% of each run, Pallas kernels for 0% -> 0%
where the time goes in v2:
time: 75.5 us; the launch traced here: 75.2 us
  Pallas kernels  68.3 us (90%)
  local copies, waits for them, and re-layouts  4.98 us (7%)
  other arithmetic  1.88 us (2%)
    pallas_call x1, Pallas kernels, on_device(): pl.pallas_call(functools.partial(kernel, n_occ, n_rep, n, domb, npno, blk...  68.3 us
    unnamed x8, local copies, waits for them, and re-layouts  1.7 us

profile of v2, /device:TPU:1, one launch (start us, length us, event | category | flops | bytes accessed | tf_op | source)
XLA Modules:
  0.0 75.2 jit_solution(1390383624391092570)
XLA Ops:
  0.0 0.0 copy-start
  0.0 0.7 multiply_add_fusion
  0.7 0.1 copy.25
  0.8 0.1 reshape.100.rids
  0.9 0.0 copy-start.1
  0.9 0.0 copy-done
  0.9 0.1 constant_dynamic-slice_fusion.1
  1.0 0.1 select_reduce_fusion
  1.1 0.7 add.64.snear
  1.8 0.1 copy.29
  1.9 0.1 copy.28
  2.0 0.1 reshape.101
  2.1 0.6 gather_fusion
  2.7 0.1 constant_dynamic-slice_fusion
  2.7 0.1 copy.26
  2.8 0.1 copy.27
  2.9 0.3 select_reduce_fusion.1
  3.3 0.1 copy.30
  3.4 0.0 copy-start.2
  3.4 0.6 add.73.sfar
  4.0 0.1 copy-done.2
  4.1 0.1 convert_reduce_fusion
  4.1 0.6 reshape.102.counts
  4.7 0.0 copy-done.1
  4.7 0.1 tile.9
  4.8 0.6 compare_select_fusion.1.ridrow
  5.4 68.3 %shard_map.82 = f32[4,4096]{1,0:T(4,128)} custom-call(s32[4]{0:T(128)} %cnt.1, s32[8]{0:T(128)} %copy-done.1, s32[512]{0:T(512)} %add.64.snear, s32[96]{0:T(128)} %add.73.sfar, f32[64]{0:T(128)} %reshape.102.counts, bf16[4,12,64,128]{3,2,1,0:T(8,128)(2,1)} %coef.1, bf16[4,96,8,128]{3,2,1,0:T(8,128)(2,1)} %bitcast.4, bf16[4,4096]{1,0:T(4,128)(2,1)} %amp.1, ...), custom_call_target="tpu_custom_call" | custom-call | tf_op jit(solution)/shard_map/pallas_call | solution.py:346
  73.8 1.5 %copy.32 = f32[4,4096]{1,0:T(4,128)} copy(f32[4,4096]{1,0:T(4,128)} %shard_map.82) | data formatting | bytes 131072
  (7 shorter events, 0.0 us)
Async XLA Ops:
  0.0 0.9 %copy-start = (s32[512,12]{0,1:T(8,128)S(1)}, s32[512,12]{0,1:T(8,128)}, u32[]{:S(2)}) copy-start(s32[512,12]{0,1:T(8,128)} %param.12) | copy-start | bytes 73732
  0.9 3.9 %copy-start.1 = (s32[8]{0:T(128)}, s32[8]{0:T(128)S(1)}, u32[]{:S(2)}) copy-start(s32[8]{0:T(128)S(1)} %reshape.100.rids) | copy-start | bytes 100
  3.4 0.7 copy-start.2

commit v3 on v2

v3 whole, which is shorter than its diff:
```python
import functools

import jax
import jax.numpy as jnp
from jax import lax
from jax.experimental import pallas as pl
from jax.experimental.pallas import tpu as pltpu
from jax.sharding import PartitionSpec as P

MESH = pl.DeviceIdType.MESH
NBLK = 32
KN = 2
BF = jnp.bfloat16
F32 = jnp.float32
NT = (((1,), (1,)), ((), ()))


def split(x):
    hi = x.astype(BF)
    return hi, (x - hi.astype(F32)).astype(BF)


def mm(a, b):
    return jnp.dot(a, b, preferred_element_type=F32)


def mm_nt(a, b):
    return lax.dot_general(a, b, NT, preferred_element_type=F32)


def kernel(
    n_occ, n_rep, n, domb, npno, blk, nx, nz,
    cnt, fown, fpair, coef, coefs, amp, den, near, dom,
    out,
    G0, G1, G2, G3, F, R1, SF, T0, TB, TP, GP, GT, RB, RT, ST, SB, FB, FT, RR, RQ, rqs, IV, ivs, acc, BD, W,
    BKs, BKr, BS, BB, X,
    ysend, yrecv, tsend, trecv, p1s, p1r, p2s, p2r, bs, br, lsem,
):
    me = lax.axis_index("occ")
    rep = lax.axis_index("rep")
    cores = n_occ // (nx * nz)
    mx, mz, mc = me // (nz * cores), lax.rem(me // cores, nz), lax.rem(me, cores)
    req = n * KN
    group = n * n_rep
    tiles = npno * npno // 128
    per = domb * npno // 8 // n_occ
    lane = lax.broadcasted_iota(jnp.int32, (8, 128), 1)
    sub = lax.broadcasted_iota(jnp.int32, (8, 128), 0)
    low = lane < npno
    G = (G0, G1, G2, G3)

    def occ_dev(d):
        return {"occ": d}

    def rep_dev(r):
        return {"rep": lax.rem(rep + r, n_rep)}

    def at(dx, dz, dc):
        return (lax.rem(mx + dx, nx) * nz + lax.rem(mz + dz, nz)) * cores + lax.rem(mc + dc, cores)

    def peer(k):
        dx, rest = lax.rem(k, nx), k // nx
        return at(dx, lax.rem(rest + dx, nz), rest // nz)

    def span(d, m):
        return min(d, m - d)

    outward = sorted(
        [(dx, dz, dc) for dc in range(cores) for dz in range(nz) for dx in range(nx) if (dx, dz, dc) != (0, 0, 0)],
        key=lambda o: -(span(o[0], nx) + span(o[1], nz)))

    barrier = pltpu.get_barrier_semaphore()
    for o in outward:
        pl.semaphore_signal(barrier, inc=1, device_id=occ_dev(at(*o)), device_id_type=MESH)
    for r in range(1, n_rep):
        pl.semaphore_signal(barrier, inc=1, device_id=rep_dev(r), device_id_type=MESH)

    blocks = pl.ds(0, domb)
    own = pltpu.make_async_copy(coef, G0.at[:, blocks], lsem.at[0])
    own.start()
    own1 = pltpu.make_async_copy(
        coefs.at[:, pl.ds(me * per, per)], R1.at[pl.ds(me * n, n)], lsem.at[1])
    own1.start()

    rr = jnp.zeros((1, 128), jnp.int32)
    lane1 = lax.broadcasted_iota(jnp.int32, (1, 128), 1)
    base = lax.rem(me * req, 128)
    for j in range(req):
        rr = jnp.where(lane1 == base + j, fown[j // KN, j % KN] * 8 + fpair[j // KN, j % KN], rr)
    RR[...] = rr
    RQ[me] = rr

    cntv = jnp.zeros((8, 128), jnp.int32)
    for p in range(n):
        cntv = jnp.where(sub == p, cnt[p], cntv)
    col = lax.rem(lane, npno)
    up = lane // npno
    pad = jnp.zeros((8 - n, 128), F32)
    last = None
    for i in range(tiles):
        x = jnp.concatenate([amp[:, 128 * i : 128 * i + 128].astype(F32), pad], axis=0)
        live = (2 * i + up < cntv) & (col < cntv)
        x = jnp.where(live, x, 0.0)
        T0[pl.ds(8 * i, 8), :] = x
        TB[i] = x.astype(BF)
        if i % 2:
            TP[i // 2] = (last + pltpu.roll(x, n, 0)).astype(BF)
        last = x

    rows_d = [dom[pl.ds(pl.multiple_of(me * group, group), group), :]]
    for j in range(req):
        owner, pair = fown[j // KN, j % KN], fpair[j // KN, j % KN]
        rows_d.append(dom[pl.ds((owner * n_rep + rep) * n + pair, 1), :])
    dd = jnp.concatenate(rows_d, axis=0)
    lane_i = lax.broadcasted_iota(jnp.int32, (group + req, 128), 1)
    inv = jnp.full((group + req, 128), domb, jnp.int32)
    for a in range(domb):
        inv = jnp.where(dd[:, a : a + 1] == lane_i, a, inv)
    IV[pl.ds(0, group + req), :] = inv
    IV[pl.ds(group + req, group), pl.ds(0, domb)] = dd[:group]

    for g in G:
        g[:, domb] = jnp.zeros((n, npno, blk), BF)
    F[:, pl.ds(domb * 8, 8)] = jnp.zeros((req, 8, 8, blk), BF)
    RB[me] = TB[me]

    pl.semaphore_wait(barrier, n_occ - 1 + n_rep - 1)
    index = pltpu.make_async_copy(IV, ivs, lsem.at[3])
    index.start()

    def plane(k, c):
        d = peer(k)
        pltpu.make_async_remote_copy(
            RR, RQ.at[me], p1s.at[0], p1r.at[0], device_id=occ_dev(d), device_id_type=MESH).start()
        pltpu.make_async_remote_copy(
            TB.at[d], RB.at[me], p1s.at[1], p1r.at[1], device_id=occ_dev(d), device_id_type=MESH).start()
        pltpu.make_async_remote_copy(
            coefs.at[:, pl.ds(d * per, per)], R1.at[pl.ds(me * n, n)], p1s.at[2], p1r.at[2],
            device_id=occ_dev(d), device_id_type=MESH).start()
        return c

    lax.fori_loop(1, n_occ, plane, 0)

    sends = {}
    for r in sorted(range(1, n_rep), key=lambda r: span(r, n_rep)):
        to = n_rep - r
        t = pltpu.make_async_remote_copy(
            TP, GP.at[to], tsend.at[r], trecv.at[to], device_id=rep_dev(r), device_id_type=MESH)
        c = pltpu.make_async_remote_copy(
            coef, G[to].at[:, blocks], ysend.at[r], yrecv.at[to], device_id=rep_dev(r), device_id_type=MESH)
        t.start()
        c.start()
        sends[r] = (t, c)

    def wait_all(ref, sem):
        pltpu.make_async_copy(ref, ref, sem).wait()

    index.wait()
    own.wait()
    GP[0] = TP[...]
    lane32 = lax.broadcasted_iota(jnp.int32, (npno // 2, 128), 1) < npno
    low64 = lax.broadcasted_iota(jnp.int32, (npno, 128), 1) < npno

    def place(x, slot, odd):
        other = pltpu.roll(x, npno, 1)
        if odd:
            BD[slot, pl.ds(npno, npno // 2, stride=2), :] = jnp.where(lane32, 0.0, other)
            BD[slot, pl.ds(npno + 1, npno // 2, stride=2), :] = jnp.where(lane32, 0.0, x)
        else:
            BD[slot, pl.ds(0, npno // 2, stride=2), :] = jnp.where(lane32, x, 0.0)
            BD[slot, pl.ds(1, npno // 2, stride=2), :] = jnp.where(lane32, other, 0.0)

    def near_part(r, gains):
        dev = lax.rem(rep + r, n_rep)
        acc[...] = jnp.zeros_like(acc)

        def overlap(b, c):
            hs, gs = [], []
            for t in range(4):
                bb = 4 * b + t
                hs.append(jnp.concatenate([G0[p, ivs[rep * n + p, bb]] for p in range(n)], axis=0))
                gs.append(jnp.concatenate([G[r][q, ivs[dev * n + q, bb]] for q in range(n)], axis=0))
            acc[...] += mm_nt(jnp.concatenate(hs, axis=1), jnp.concatenate(gs, axis=1))
            return c

        lax.fori_loop(0, NBLK // 4, overlap, 0)
        GT[...] = GP[r].astype(F32).reshape(n * tiles, 128)
        for q in range(n):
            place(GT[pl.ds(q, npno // 2, stride=n), :], (n * r + q) // 2, q % 2)
        parts = [[] for _ in range(n)]
        for k in range(n // 2):
            hi, lo = split(acc[:, 128 * k : 128 * k + 128])
            bd = BD[n // 2 * r + k].astype(BF)
            u = mm(jnp.concatenate([hi, lo], axis=1), jnp.concatenate([bd, bd], axis=0))
            q = dev * n + 2 * k
            c0 = jnp.sum((near[...] == q).astype(F32), axis=1, keepdims=True)
            c1 = jnp.sum((near[...] == q + 1).astype(F32), axis=1, keepdims=True)
            w = jnp.where(low[:n], c0, c1)
            for p in range(n):
                rows = slice(p * npno, (p + 1) * npno)
                uh, ul = split(u[rows] * w[p : p + 1])
                parts[p].append((uh, ul, hi[rows], lo[rows]))
        for p in range(n):
            uh, ul, sh, sl = (jnp.concatenate(v, axis=1) for v in zip(*parts[p]))
            g = mm_nt(uh, sh) + mm_nt(ul, sh) + mm_nt(uh, sl)
            if gains:
                g = g + W[2 * req + p, :, pl.ds(0, npno)]
            W[2 * req + p, :, pl.ds(0, npno)] = g

    near_part(0, False)

    wait_all(RQ.at[pl.ds(0, n_occ - 1)], p1r.at[0])
    table = pltpu.make_async_copy(RQ, rqs, lsem.at[2])
    table.start()
    wait_all(RB.at[pl.ds(0, n_occ - 1)], p1r.at[1])
    RT[...] = RB[...].astype(F32).reshape(8 * n_occ, 128)
    wait_all(R1.at[pl.ds(0, n * (n_occ - 1))], p1r.at[2])
    own1.wait()
    table.wait()

    def pick(d, j):
        r = rqs[d, 0, lax.rem(d * req + j, 128)]
        return r, r - (r >> 3) * (8 - n)

    for j in range(req):
        r8, r4 = pick(me, j)
        F[j, pl.ds(me * per, per)] = R1[r4]
        ST[pl.ds(8 * me + j, 1), :] = RT[pl.ds(r8, 1), :]
    FB[me] = ST[pl.ds(8 * me, 8), :].astype(BF)

    def gather(d):
        for j in range(req):
            r8, r4 = pick(d, j)
            SF[d, j] = R1[r4]
            ST[pl.ds(8 * d + j, 1), :] = RT[pl.ds(r8, 1), :]
        SB[d] = ST[pl.ds(8 * d, 8), :].astype(BF)

    def ship(d):
        pltpu.make_async_remote_copy(
            SF.at[d], F.at[:, pl.ds(me * per, per)], p2s.at[0], p2r.at[0],
            device_id=occ_dev(d), device_id_type=MESH).start()
        pltpu.make_async_remote_copy(
            SB.at[d], FB.at[me], p2s.at[1], p2r.at[1],
            device_id=occ_dev(d), device_id_type=MESH).start()

    gather(peer(1))

    def answer(k, c):
        gather(peer(k))
        ship(peer(k - 1))
        return c

    lax.fori_loop(2, n_occ, answer, 0)
    ship(peer(n_occ - 1))

    for r in sorted(range(1, n_rep), key=lambda r: span(r, n_rep)):
        for c in sends[n_rep - r]:
            c.wait_recv()
        near_part(r, True)

    wait_all(FB.at[pl.ds(0, n_occ - 1)], p2r.at[1])
    FT[...] = FB[...].astype(F32).reshape(8 * n_occ, 128)
    for j in range(req):
        place(FT[pl.ds(j, npno // 2, stride=8), :], (group + j) // 2, j % 2)
    wait_all(F.at[:, pl.ds(0, (n_occ - 1) * per)], p2r.at[0])

    def flat(slot):
        e = W[slot, pl.ds(0, npno // 2, stride=2), :]
        o = W[slot, pl.ds(1, npno // 2, stride=2), :]
        return jnp.where(lane32, e, pltpu.roll(o, npno, 1))

    z = jnp.zeros((npno, 128), BF)
    for p in range(n):
        h = jnp.concatenate([G0[p, a] for a in range(domb)], axis=1)
        f = jnp.concatenate([
            jnp.concatenate([
                F[j, pl.ds(8 * ivs[group + j, ivs[group + req + rep * n + p, a]], 8)].reshape(npno, blk)
                for a in range(domb)], axis=1)
            for j in range(KN * p, KN * p + KN)], axis=0)
        s = mm_nt(h, f)
        sh, sl = split(s)
        th, tl = split(s.T)
        bd = BD[group // 2 + p].astype(BF)
        u = mm(jnp.concatenate([sh, sl], axis=1), jnp.concatenate([bd, bd], axis=0))
        odd = p % 2
        tp = BD[p // 2, pl.ds(odd * npno, npno), :].astype(BF)
        v = mm(jnp.concatenate([tp, tp], axis=1),
               jnp.concatenate([z, sh, z, sl] if odd else [sh, z, sl, z], axis=0))
        vh, vl = split(v)
        b = mm(th, vh) + mm(tl, vh) + mm(th, vl)
        W[KN * p, :, :] = b[:npno]
        W[KN * p + 1, :, :] = pltpu.roll(b[npno:], npno, 1)
        uh, ul = split(u)
        W[2 * req + p, :, pl.ds(0, npno)] += mm_nt(uh, sh) + mm_nt(ul, sh) + mm_nt(uh, sl)
    for j in range(req):
        BKs[pl.ds(j, npno // 2, stride=8), :] = flat(j)

    def back(src, dst, s):
        for o in outward:
            d = at(*o)
            pltpu.make_async_remote_copy(
                src.at[pl.ds(8 * d, 8)], dst.at[pl.ds(8 * me, 8)], bs.at[s], br.at[s],
                device_id=occ_dev(d), device_id_type=MESH).start()
        dst[pl.ds(8 * me, 8), :] = src[pl.ds(8 * me, 8), :]

    rows_in = pl.ds(0, 8 * (n_occ - 1))
    back(BKs, BKr, 0)
    hn = n_occ // 2
    ids = jnp.concatenate(
        [jnp.sum(RQ[pl.ds(h * hn, hn)], axis=0) for h in range(2)], axis=1)
    hot = (lax.broadcasted_iota(jnp.int32, (8 * n_occ, req * n_occ), 0) == ids).astype(F32).astype(BF)
    for p in range(n):
        X[pl.ds(p, npno // 2, stride=8), :] = flat(2 * req + p)
    de = jnp.concatenate([den[...], jnp.zeros((8 - n, npno), F32)], axis=0)
    db = jnp.concatenate([de, de], axis=1)
    for i in range(tiles):
        r = pl.ds(8 * i, 8)
        da = jnp.where(low, de[:, 2 * i : 2 * i + 1], de[:, 2 * i + 1 : 2 * i + 2])
        X[r, :] = (da + db) * T0[r, :] + X[r, :]
    wait_all(BKr.at[rows_in], br.at[0])
    kh, kl = split(BKr[...])
    BS[...] = mm(hot, kh) + mm(hot, kl)
    back(BS, BB, 1)
    wait_all(BB.at[rows_in], br.at[1])
    for i in range(tiles):
        r = pl.ds(8 * i, 8)
        live = (2 * i + up < cntv) & (col < cntv)
        out[:, 128 * i : 128 * i + 128] = jnp.where(live, X[r, :] + BB[r, :], 0.0)[:n]

    for r in range(1, n_rep):
        for c in sends[r]:
            c.wait_send()
    wait_all(RQ.at[pl.ds(0, n_occ - 1)], p1s.at[0])
    wait_all(RB.at[pl.ds(0, n_occ - 1)], p1s.at[1])
    wait_all(R1.at[pl.ds(0, n * (n_occ - 1))], p1s.at[2])
    wait_all(F.at[:, pl.ds(0, (n_occ - 1) * per)], p2s.at[0])
    wait_all(FB.at[pl.ds(0, n_occ - 1)], p2s.at[1])
    wait_all(BKr.at[rows_in], bs.at[0])
    wait_all(BB.at[rows_in], bs.at[1])


def on_device(n_occ, n_rep, coeffs, amplitudes, denominators, pno_count, domains, far_owner, far_pair, near_pair):
    n, domb, npno, blk = coeffs.shape
    group = n * n_rep
    req = n * KN
    i32 = jnp.int32
    smem = pl.BlockSpec(memory_space=pltpu.SMEM)
    vmem = pl.BlockSpec(memory_space=pltpu.VMEM)
    anym = pl.BlockSpec(memory_space=pl.ANY)
    rows = 8 * n_occ
    per = domb * npno // 8 // n_occ
    tiles = npno * npno // 128
    V = pltpu.VMEM
    dma = pltpu.SemaphoreType.DMA
    return pl.pallas_call(
        functools.partial(kernel, n_occ, n_rep, n, domb, npno, blk, 4, 4),
        out_shape=jax.ShapeDtypeStruct((n, npno * npno), F32),
        in_specs=[smem] * 3 + [anym, anym] + [vmem] * 4,
        out_specs=vmem,
        scratch_shapes=[V((n, domb + 1, npno, blk), BF)] * 4 + [
            V((req, (domb + 1) * 8, 8, blk), BF),
            V((n_occ * n, per, 8, blk), BF),
            V((n_occ, req, per, 8, blk), BF),
            V((rows, 128), F32),
            V((n_occ, 8, 128), BF),
            V((tiles // 2, 8, 128), BF),
            V((n_rep, tiles // 2, 8, 128), BF),
            V((n * tiles, 128), F32),
            V((n_occ, 8, 128), BF),
            V((rows, 128), F32),
            V((rows, 128), F32),
            V((n_occ, 8, 128), BF),
            V((n_occ, 8, 128), BF),
            V((rows, 128), F32),
            V((1, 128), i32),
            V((n_occ, 1, 128), i32),
            pltpu.SMEM((n_occ, 1, 128), i32),
            V((2 * group + req, 128), i32),
            pltpu.SMEM((2 * group + req, 128), i32),
            V((n * npno, n * npno), F32),
            V((group // 2 + n, 128, 128), F32),
            V((2 * req + n, npno, 128), F32),
            V((rows, 128), F32),
            V((rows, 128), F32),
            V((rows, 128), F32),
            V((rows, 128), F32),
            V((rows, 128), F32),
            dma((n_rep,)), dma((n_rep,)), dma((n_rep,)), dma((n_rep,)),
            dma((3,)), dma((3,)), dma((2,)), dma((2,)), dma((2,)), dma((2,)), dma((4,)),
        ],
        compiler_params=pltpu.CompilerParams(
            collective_id=0, has_side_effects=True, vmem_limit_bytes=56 * 1024 * 1024),
    )(pno_count, far_owner, far_pair, coeffs, coeffs.reshape(n, domb * npno // 8, 8, blk),
      amplitudes, denominators, near_pair, domains)


def solution(mesh):
    both = ("occ", "rep")
    in_specs = (
        P(both, None, None, None), P(both, None), P(both, None), P(both),
        P(), P(both, None), P(both, None), P(both, None),
    )
    return jax.shard_map(
        functools.partial(on_device, mesh.shape["occ"], mesh.shape["rep"]),
        mesh=mesh, in_specs=in_specs, out_specs=P(both, None), check_vma=False,
    )
```

time: 75.5 us -> 70.4 us (0.932)
  Pallas kernels: 68.3 us -> 65 us
  other arithmetic: 1.88 us -> 0 us
    unnamed x8, local copies, waits for them, and re-layouts: 1.7 us -> 5.06 us
    pallas_call x1, Pallas kernels: 68.3 us -> 65 us  [on_device(): pl.pallas_call(functools.partial(kernel, n_occ, n_rep, n, domb, npno, blk...]
    add x4 -> x0, local copies, waits for them, and re-layouts: 1.45 us -> none  [the longest x1 0.66 us: on_device(): snear = (domb + jnp.sum(jnp.where(hot, a_id, 0), axis=2)).reshape(-1)]
    reshape x3 -> x0, local copies, waits for them, and re-layouts: 0.76 us -> none  [the longest x1 0.59 us: on_device(): counts.reshape(-1)]
where the time goes in v3:
time: 70.4 us; the launch traced here: 70.1 us
  Pallas kernels  65 us (92%)
  local copies, waits for them, and re-layouts  5.06 us (7%)
    pallas_call x1, Pallas kernels, on_device(): pl.pallas_call(functools.partial(kernel, n_occ, n_rep, n, domb, npno, blk...  65 us
    unnamed x8, local copies, waits for them, and re-layouts  5.06 us

profile of v3, /device:TPU:1, one launch (start us, length us, event | category | flops | bytes accessed | tf_op | source)
XLA Modules:
  0.0 70.1 jit_solution(1377087046744692973)
XLA Ops:
  0.0 0.0 copy-start
  0.0 0.7 copy-done
  0.7 0.0 copy-start.1
  0.7 0.7 copy.9.fown
  1.3 0.0 copy-done.1
  1.4 0.6 copy.10.fpair
  2.0 1.6 %copy.11.dom = s32[512,12]{1,0:T(8,128)} copy(s32[512,12]{0,1:T(8,128)} %param.12) | data formatting | bytes 49152 | tf_op args[4]
  3.6 65.0 %shard_map.82 = f32[4,4096]{1,0:T(4,128)} custom-call(s32[4]{0:T(128)} %cnt.1, s32[4,2]{1,0:T(4,128)} %copy.9.fown, s32[4,2]{1,0:T(4,128)} %copy.10.fpair, bf16[4,12,64,128]{3,2,1,0:T(8,128)(2,1)} %coef.1, bf16[4,96,8,128]{3,2,1,0:T(8,128)(2,1)} %bitcast.1, bf16[4,4096]{1,0:T(4,128)(2,1)} %amp.1, f32[4,64]{1,0:T(4,128)} %den.1, s32[4,40]{1,0:T(4,128)} %near.1, ...), custom_call_target="tpu_custom_call" | custom-call | tf_op jit(solution)/shard_map/pallas_call | solution.py:355
  68.6 1.5 %copy.13 = f32[4,4096]{1,0:T(4,128)} copy(f32[4,4096]{1,0:T(4,128)} %shard_map.82) | data formatting | bytes 131072
Async XLA Ops:
  0.0 0.7 copy-start
  0.7 0.7 copy-start.1

commit v4 on v3

--- a/solution.py
+++ b/solution.py
@@ -32,7 +32,7 @@
     n_occ, n_rep, n, domb, npno, blk, nx, nz,
     cnt, fown, fpair, coef, coefs, amp, den, near, dom,
     out,
-    G0, G1, G2, G3, F, R1, SF, T0, TB, TP, GP, GT, RB, RT, ST, SB, FB, FT, RR, RQ, rqs, IV, ivs, acc, BD, W,
+    G0, G1, G2, G3, F, PS, R1, SF, T0, TP, GP, GT, RT, ST, FT, RR, RQ, rqs, DT, IV, ivs, acc, BD, W,
     BKs, BKr, BS, BB, X,
     ysend, yrecv, tsend, trecv, p1s, p1r, p2s, p2r, bs, br, lsem,
 ):
@@ -78,15 +78,17 @@
     blocks = pl.ds(0, domb)
     own = pltpu.make_async_copy(coef, G0.at[:, blocks], lsem.at[0])
     own.start()
-    own1 = pltpu.make_async_copy(
-        coefs.at[:, pl.ds(me * per, per)], R1.at[pl.ds(me * n, n)], lsem.at[1])
-    own1.start()
+    cuts = [
+        pltpu.make_async_copy(coefs.at[p, t], PS.at[:, per * p + t], lsem.at[4 + per * p + t])
+        for p in range(n) for t in range(per)]
+    for c in cuts:
+        c.start()
 
     rr = jnp.zeros((1, 128), jnp.int32)
     lane1 = lax.broadcasted_iota(jnp.int32, (1, 128), 1)
     base = lax.rem(me * req, 128)
     for j in range(req):
-        rr = jnp.where(lane1 == base + j, fown[j // KN, j % KN] * 8 + fpair[j // KN, j % KN], rr)
+        rr = jnp.where(lane1 == base + j, fown[j % KN, j // KN] * 8 + fpair[j % KN, j // KN], rr)
     RR[...] = rr
     RQ[me] = rr
 
@@ -102,55 +104,81 @@
         live = (2 * i + up < cntv) & (col < cntv)
         x = jnp.where(live, x, 0.0)
         T0[pl.ds(8 * i, 8), :] = x
-        TB[i] = x.astype(BF)
+        PS[i, n * per] = x.astype(BF)
         if i % 2:
             TP[i // 2] = (last + pltpu.roll(x, n, 0)).astype(BF)
         last = x
 
-    rows_d = [dom[pl.ds(pl.multiple_of(me * group, group), group), :]]
+    dt = jnp.concatenate([dom[...], jnp.zeros((-domb % 8, dom.shape[1]), jnp.int32)], axis=0)
+    DT[...] = dt.T
+    rows_d = [DT[pl.ds(pl.multiple_of(me * group, group), group), :]]
     for j in range(req):
-        owner, pair = fown[j // KN, j % KN], fpair[j // KN, j % KN]
-        rows_d.append(dom[pl.ds((owner * n_rep + rep) * n + pair, 1), :])
+        owner, pair = fown[j % KN, j // KN], fpair[j % KN, j // KN]
+        rows_d.append(DT[pl.ds((owner * n_rep + rep) * n + pair, 1), :])
     dd = jnp.concatenate(rows_d, axis=0)
     lane_i = lax.broadcasted_iota(jnp.int32, (group + req, 128), 1)
     inv = jnp.full((group + req, 128), domb, jnp.int32)
     for a in range(domb):
         inv = jnp.where(dd[:, a : a + 1] == lane_i, a, inv)
-    IV[pl.ds(0, group + req), :] = inv
-    IV[pl.ds(group + req, group), pl.ds(0, domb)] = dd[:group]
+    IV[pl.ds(0, group), :] = inv[:group]
+    fi = inv[group:]
+    have = fi < domb
+    IV[pl.ds(group, req), :] = jnp.where(have, lax.rem(fi * 8, n_occ), n_occ)
+    IV[pl.ds(group + req, req), :] = jnp.where(have, (fi * 8) // n_occ, 0)
+    IV[pl.ds(group + 2 * req, group), pl.ds(0, dd.shape[1])] = dd[:group]
 
     for g in G:
         g[:, domb] = jnp.zeros((n, npno, blk), BF)
-    F[:, pl.ds(domb * 8, 8)] = jnp.zeros((req, 8, 8, blk), BF)
-    RB[me] = TB[me]
+    for j in range(req):
+        F[pl.ds(n_occ, 8), per * j] = jnp.zeros((8, 8, blk), BF)
+    for c in cuts:
+        c.wait()
+    R1[me] = PS[me]
 
     pl.semaphore_wait(barrier, n_occ - 1 + n_rep - 1)
     index = pltpu.make_async_copy(IV, ivs, lsem.at[3])
     index.start()
 
-    def plane(k, c):
-        d = peer(k)
+    half = n // 2
+    ahead, behind = 1, n_rep - 1
+    opposite = n_rep // 2
+
+    def halfway(src, h, to, r, s):
+        return pltpu.make_async_remote_copy(
+            src, G[to].at[pl.ds(h * half, half), blocks], ysend.at[s], yrecv.at[s],
+            device_id=rep_dev(r), device_id_type=MESH)
+
+    firsts = [
+        halfway(coef.at[pl.ds(0, half)], 0, behind, ahead, 0),
+        halfway(coef.at[pl.ds(half, half)], 1, ahead, behind, 1),
+        halfway(coef.at[pl.ds(half, half)], 1, behind, ahead, 2),
+        halfway(coef.at[pl.ds(0, half)], 0, ahead, behind, 3)]
+    relays = [
+        halfway(G[behind].at[pl.ds(0, half), blocks], 0, opposite, ahead, 4),
+        halfway(G[ahead].at[pl.ds(half, half), blocks], 1, opposite, behind, 5)]
+    firsts[0].start()
+    firsts[1].start()
+    amps = []
+    for r in range(1, n_rep):
+        t = pltpu.make_async_remote_copy(
+            TP, GP.at[n_rep - r], tsend.at[r], trecv.at[n_rep - r], device_id=rep_dev(r), device_id_type=MESH)
+        t.start()
+        amps.append(t)
+    firsts[2].start()
+    firsts[3].start()
+
+    def slices(o):
+        d = at(*o)
         pltpu.make_async_remote_copy(
-            RR, RQ.at[me], p1s.at[0], p1r.at[0], device_id=occ_dev(d), device_id_type=MESH).start()
+            PS.at[d], R1.at[me], p1s.at[1], p1r.at[1], device_id=occ_dev(d), device_id_type=MESH).start()
+
+    for o in outward[:8]:
+        slices(o)
+    for o in outward:
         pltpu.make_async_remote_copy(
-            TB.at[d], RB.at[me], p1s.at[1], p1r.at[1], device_id=occ_dev(d), device_id_type=MESH).start()
-        pltpu.make_async_remote_copy(
-            coefs.at[:, pl.ds(d * per, per)], R1.at[pl.ds(me * n, n)], p1s.at[2], p1r.at[2],
-            device_id=occ_dev(d), device_id_type=MESH).start()
-        return c
-
-    lax.fori_loop(1, n_occ, plane, 0)
-
-    sends = {}
-    for r in sorted(range(1, n_rep), key=lambda r: span(r, n_rep)):
-        to = n_rep - r
-        t = pltpu.make_async_remote_copy(
-            TP, GP.at[to], tsend.at[r], trecv.at[to], device_id=rep_dev(r), device_id_type=MESH)
-        c = pltpu.make_async_remote_copy(
-            coef, G[to].at[:, blocks], ysend.at[r], yrecv.at[to], device_id=rep_dev(r), device_id_type=MESH)
-        t.start()
-        c.start()
-        sends[r] = (t, c)
+            RR, RQ.at[me], p1s.at[0], p1r.at[0], device_id=occ_dev(at(*o)), device_id_type=MESH).start()
+    for o in outward[8:]:
+        slices(o)
 
     def wait_all(ref, sem):
         pltpu.make_async_copy(ref, ref, sem).wait()
@@ -212,70 +240,64 @@
     wait_all(RQ.at[pl.ds(0, n_occ - 1)], p1r.at[0])
     table = pltpu.make_async_copy(RQ, rqs, lsem.at[2])
     table.start()
-    wait_all(RB.at[pl.ds(0, n_occ - 1)], p1r.at[1])
-    RT[...] = RB[...].astype(F32).reshape(8 * n_occ, 128)
-    wait_all(R1.at[pl.ds(0, n * (n_occ - 1))], p1r.at[2])
-    own1.wait()
+    wait_all(R1.at[pl.ds(0, n_occ - 1)], p1r.at[1])
+    RT[...] = R1[:, n * per].astype(F32).reshape(8 * n_occ, 128)
     table.wait()
 
-    def pick(d, j):
-        r = rqs[d, 0, lax.rem(d * req + j, 128)]
-        return r, r - (r >> 3) * (8 - n)
-
-    for j in range(req):
-        r8, r4 = pick(me, j)
-        F[j, pl.ds(me * per, per)] = R1[r4]
-        ST[pl.ds(8 * me + j, 1), :] = RT[pl.ds(r8, 1), :]
-    FB[me] = ST[pl.ds(8 * me, 8), :].astype(BF)
-
-    def gather(d):
+    def gather(d, dst, at_d):
         for j in range(req):
-            r8, r4 = pick(d, j)
-            SF[d, j] = R1[r4]
-            ST[pl.ds(8 * d + j, 1), :] = RT[pl.ds(r8, 1), :]
-        SB[d] = ST[pl.ds(8 * d, 8), :].astype(BF)
+            r = rqs[d, 0, lax.rem(d * req + j, 128)]
+            dst[at_d, pl.ds(per * j, per)] = R1[r >> 3, pl.ds(per * (r & 7), per)]
+            ST[pl.ds(8 * d + j, 1), :] = RT[pl.ds(r, 1), :]
+        dst[at_d, req * per] = ST[pl.ds(8 * d, 8), :].astype(BF)
 
     def ship(d):
         pltpu.make_async_remote_copy(
-            SF.at[d], F.at[:, pl.ds(me * per, per)], p2s.at[0], p2r.at[0],
-            device_id=occ_dev(d), device_id_type=MESH).start()
-        pltpu.make_async_remote_copy(
-            SB.at[d], FB.at[me], p2s.at[1], p2r.at[1],
-            device_id=occ_dev(d), device_id_type=MESH).start()
-
-    gather(peer(1))
+            SF.at[d], F.at[me], p2s.at[0], p2r.at[0], device_id=occ_dev(d), device_id_type=MESH).start()
+
+    gather(peer(1), SF, peer(1))
 
     def answer(k, c):
-        gather(peer(k))
+        gather(peer(k), SF, peer(k))
         ship(peer(k - 1))
         return c
 
     lax.fori_loop(2, n_occ, answer, 0)
     ship(peer(n_occ - 1))
-
-    for r in sorted(range(1, n_rep), key=lambda r: span(r, n_rep)):
-        for c in sends[n_rep - r]:
-            c.wait_recv()
-        near_part(r, True)
-
-    wait_all(FB.at[pl.ds(0, n_occ - 1)], p2r.at[1])
-    FT[...] = FB[...].astype(F32).reshape(8 * n_occ, 128)
+    gather(me, F, me)
+
+    for t in range(2):
+        firsts[t].wait_recv()
+        relays[t].start()
+    for t in amps:
+        t.wait_recv()
+    firsts[3].wait_recv()
+    near_part(ahead, True)
+    firsts[2].wait_recv()
+    near_part(behind, True)
+    for t in relays:
+        t.wait_recv()
+    near_part(opposite, True)
+
+    wait_all(F.at[pl.ds(0, n_occ - 1)], p2r.at[0])
+    FT[...] = F[pl.ds(0, n_occ), req * per].astype(F32).reshape(8 * n_occ, 128)
     for j in range(req):
         place(FT[pl.ds(j, npno // 2, stride=8), :], (group + j) // 2, j % 2)
-    wait_all(F.at[:, pl.ds(0, (n_occ - 1) * per)], p2r.at[0])
 
     def flat(slot):
         e = W[slot, pl.ds(0, npno // 2, stride=2), :]
         o = W[slot, pl.ds(1, npno // 2, stride=2), :]
         return jnp.where(lane32, e, pltpu.roll(o, npno, 1))
 
+    def block(j, p, a):
+        b = ivs[group + 2 * req + rep * n + p, a]
+        return F[pl.ds(ivs[group + j, b], 8), per * j + ivs[group + req + j, b]].reshape(npno, blk)
+
     z = jnp.zeros((npno, 128), BF)
     for p in range(n):
         h = jnp.concatenate([G0[p, a] for a in range(domb)], axis=1)
         f = jnp.concatenate([
-            jnp.concatenate([
-                F[j, pl.ds(8 * ivs[group + j, ivs[group + req + rep * n + p, a]], 8)].reshape(npno, blk)
-                for a in range(domb)], axis=1)
+            jnp.concatenate([block(j, p, a) for a in range(domb)], axis=1)
             for j in range(KN * p, KN * p + KN)], axis=0)
         s = mm_nt(h, f)
         sh, sl = split(s)
@@ -327,14 +349,11 @@
         live = (2 * i + up < cntv) & (col < cntv)
         out[:, 128 * i : 128 * i + 128] = jnp.where(live, X[r, :] + BB[r, :], 0.0)[:n]
 
-    for r in range(1, n_rep):
-        for c in sends[r]:
-            c.wait_send()
+    for c in firsts + relays + amps:
+        c.wait_send()
     wait_all(RQ.at[pl.ds(0, n_occ - 1)], p1s.at[0])
-    wait_all(RB.at[pl.ds(0, n_occ - 1)], p1s.at[1])
-    wait_all(R1.at[pl.ds(0, n * (n_occ - 1))], p1s.at[2])
-    wait_all(F.at[:, pl.ds(0, (n_occ - 1) * per)], p2s.at[0])
-    wait_all(FB.at[pl.ds(0, n_occ - 1)], p2s.at[1])
+    wait_all(R1.at[pl.ds(0, n_occ - 1)], p1s.at[1])
+    wait_all(F.at[pl.ds(0, n_occ - 1)], p2s.at[0])
     wait_all(BKr.at[rows_in], bs.at[0])
     wait_all(BB.at[rows_in], bs.at[1])
 
@@ -358,25 +377,23 @@
         in_specs=[smem] * 3 + [anym, anym] + [vmem] * 4,
         out_specs=vmem,
         scratch_shapes=[V((n, domb + 1, npno, blk), BF)] * 4 + [
-            V((req, (domb + 1) * 8, 8, blk), BF),
-            V((n_occ * n, per, 8, blk), BF),
-            V((n_occ, req, per, 8, blk), BF),
-            V((rows, 128), F32),
-            V((n_occ, 8, 128), BF),
+            V((n_occ + 8, req * per + 1, 8, blk), BF),
+            V((n_occ, n * per + 1, 8, blk), BF),
+            V((n_occ, n * per + 1, 8, blk), BF),
+            V((n_occ, req * per + 1, 8, blk), BF),
+            V((rows, 128), F32),
             V((tiles // 2, 8, 128), BF),
             V((n_rep, tiles // 2, 8, 128), BF),
             V((n * tiles, 128), F32),
-            V((n_occ, 8, 128), BF),
-            V((rows, 128), F32),
-            V((rows, 128), F32),
-            V((n_occ, 8, 128), BF),
-            V((n_occ, 8, 128), BF),
+            V((rows, 128), F32),
+            V((rows, 128), F32),
             V((rows, 128), F32),
             V((1, 128), i32),
             V((n_occ, 1, 128), i32),
             pltpu.SMEM((n_occ, 1, 128), i32),
-            V((2 * group + req, 128), i32),
-            pltpu.SMEM((2 * group + req, 128), i32),
+            V((domains.shape[0], domb + -domb % 8), i32),
+            V((2 * group + 2 * req, 128), i32),
+            pltpu.SMEM((2 * group + 2 * req, 128), i32),
             V((n * npno, n * npno), F32),
             V((group // 2 + n, 128, 128), F32),
             V((2 * req + n, npno, 128), F32),
@@ -385,13 +402,13 @@
             V((rows, 128), F32),
             V((rows, 128), F32),
             V((rows, 128), F32),
-            dma((n_rep,)), dma((n_rep,)), dma((n_rep,)), dma((n_rep,)),
-            dma((3,)), dma((3,)), dma((2,)), dma((2,)), dma((2,)), dma((2,)), dma((4,)),
+            dma((6,)), dma((6,)), dma((n_rep,)), dma((n_rep,)),
+            dma((2,)), dma((2,)), dma((1,)), dma((1,)), dma((2,)), dma((2,)), dma((4 + n * per,)),
         ],
         compiler_params=pltpu.CompilerParams(
             collective_id=0, has_side_effects=True, vmem_limit_bytes=56 * 1024 * 1024),
-    )(pno_count, far_owner, far_pair, coeffs, coeffs.reshape(n, domb * npno // 8, 8, blk),
-      amplitudes, denominators, near_pair, domains)
+    )(pno_count, far_owner.T, far_pair.T, coeffs, coeffs.reshape(n, per, n_occ, 8, blk),
+      amplitudes, denominators, near_pair, domains.T)
 
 
 def solution(mesh):

time: 70.4 us -> 58.8 us (0.84)
  Pallas kernels: 65 us -> 57 us
  local copies, waits for them, and re-layouts: 5.06 us -> 1.47 us
    pallas_call x1, Pallas kernels: 65 us -> 57 us  [on_device(): pl.pallas_call(functools.partial(kernel, n_occ, n_rep, n, domb, npno, blk...]
    unnamed x8 -> x1, local copies, waits for them, and re-layouts: 5.06 us -> 1.47 us
where the time goes in v4:
time: 58.8 us; the launch traced here: 58.5 us
  Pallas kernels  57 us (97%)
  local copies, waits for them, and re-layouts  1.47 us (2%)
    pallas_call x1, Pallas kernels, on_device(): pl.pallas_call(functools.partial(kernel, n_occ, n_rep, n, domb, npno, blk...  57 us
    unnamed x1, local copies, waits for them, and re-layouts  1.47 us

profile of v4, /device:TPU:1, one launch (start us, length us, event | category | flops | bytes accessed | tf_op | source)
XLA Modules:
  0.0 58.5 jit_solution(13615002181943033791)
XLA Ops:
  0.0 57.0 %shard_map.82 = f32[4,4096]{1,0:T(4,128)} custom-call(s32[4]{0:T(128)} %cnt.1, s32[2,4]{1,0:T(2,128)} %bitcast.6, s32[2,4]{1,0:T(2,128)} %bitcast.7, bf16[4,12,64,128]{3,2,1,0:T(8,128)(2,1)} %coef.1, bf16[4,3,32,8,128]{4,3,2,1,0:T(8,128)(2,1)} %bitcast.4, bf16[4,4096]{1,0:T(4,128)(2,1)} %amp.1, f32[4,64]{1,0:T(4,128)} %den.1, s32[4,40]{1,0:T(4,128)} %near.1, ...), custom_call_target="tpu_custom_call" | custom-call | tf_op jit(solution)/shard_map/pallas_call | solution.py:374
  57.0 1.5 %copy.10 = f32[4,4096]{1,0:T(4,128)} copy(f32[4,4096]{1,0:T(4,128)} %shard_map.82) | data formatting | bytes 131072

commit v5 on v4

--- a/solution.py
+++ b/solution.py
@@ -32,7 +32,7 @@
     n_occ, n_rep, n, domb, npno, blk, nx, nz,
     cnt, fown, fpair, coef, coefs, amp, den, near, dom,
     out,
-    G0, G1, G2, G3, F, PS, R1, SF, T0, TP, GP, GT, RT, ST, FT, RR, RQ, rqs, DT, IV, ivs, acc, BD, W,
+    G0, G1, G2, G3, F, PS, RA, RZ, SF, T0, TP, GP, GT, RT, ST, FT, RR, RQ, rqs, DT, IV, ivs, acc, BD, W,
     BKs, BKr, BS, BB, X,
     ysend, yrecv, tsend, trecv, p1s, p1r, p2s, p2r, bs, br, lsem,
 ):
@@ -79,7 +79,7 @@
     own = pltpu.make_async_copy(coef, G0.at[:, blocks], lsem.at[0])
     own.start()
     cuts = [
-        pltpu.make_async_copy(coefs.at[p, t], PS.at[:, per * p + t], lsem.at[4 + per * p + t])
+        pltpu.make_async_copy(coefs.at[p, t], PS.at[:, n * t + p], lsem.at[4 + per * p + t])
         for p in range(n) for t in range(per)]
     for c in cuts:
         c.start()
@@ -130,10 +130,11 @@
     for g in G:
         g[:, domb] = jnp.zeros((n, npno, blk), BF)
     for j in range(req):
-        F[pl.ds(n_occ, 8), per * j] = jnp.zeros((8, 8, blk), BF)
+        F[pl.ds(n_occ, 8), j] = jnp.zeros((8, 8, blk), BF)
     for c in cuts:
         c.wait()
-    R1[me] = PS[me]
+    RA[me] = PS[me, pl.ds(0, n)]
+    RZ[me] = PS[me, pl.ds(n, n * (per - 1) + 1)]
 
     pl.semaphore_wait(barrier, n_occ - 1 + n_rep - 1)
     index = pltpu.make_async_copy(IV, ivs, lsem.at[3])
@@ -167,18 +168,22 @@
     firsts[2].start()
     firsts[3].start()
 
-    def slices(o):
+    def slices(o, piece):
         d = at(*o)
+        part, to = (pl.ds(n, n * (per - 1) + 1), RZ) if piece else (pl.ds(0, n), RA)
         pltpu.make_async_remote_copy(
-            PS.at[d], R1.at[me], p1s.at[1], p1r.at[1], device_id=occ_dev(d), device_id_type=MESH).start()
+            PS.at[d, part], to.at[me], p1s.at[1 + piece], p1r.at[1 + piece],
+            device_id=occ_dev(d), device_id_type=MESH).start()
 
     for o in outward[:8]:
-        slices(o)
+        slices(o, 0)
     for o in outward:
         pltpu.make_async_remote_copy(
             RR, RQ.at[me], p1s.at[0], p1r.at[0], device_id=occ_dev(at(*o)), device_id_type=MESH).start()
     for o in outward[8:]:
-        slices(o)
+        slices(o, 0)
+    for o in outward:
+        slices(o, 1)
 
     def wait_all(ref, sem):
         pltpu.make_async_copy(ref, ref, sem).wait()
@@ -240,46 +245,59 @@
     wait_all(RQ.at[pl.ds(0, n_occ - 1)], p1r.at[0])
     table = pltpu.make_async_copy(RQ, rqs, lsem.at[2])
     table.start()
-    wait_all(R1.at[pl.ds(0, n_occ - 1)], p1r.at[1])
-    RT[...] = R1[:, n * per].astype(F32).reshape(8 * n_occ, 128)
     table.wait()
-
-    def gather(d, dst, at_d):
+    others = pl.ds(0, n_occ - 1)
+    cut = (pl.ds(0, req), pl.ds(req, req * (per - 1) + 1))
+
+    def gather(d, dst, piece):
         for j in range(req):
             r = rqs[d, 0, lax.rem(d * req + j, 128)]
-            dst[at_d, pl.ds(per * j, per)] = R1[r >> 3, pl.ds(per * (r & 7), per)]
-            ST[pl.ds(8 * d + j, 1), :] = RT[pl.ds(r, 1), :]
-        dst[at_d, req * per] = ST[pl.ds(8 * d, 8), :].astype(BF)
-
-    def ship(d):
+            src, pair = r >> 3, r & 7
+            if piece:
+                for t in range(per - 1):
+                    dst[d, req * (t + 1) + j] = RZ[src, n * t + pair]
+                ST[pl.ds(8 * d + j, 1), :] = RT[pl.ds(r, 1), :]
+            else:
+                dst[d, j] = RA[src, pair]
+        if piece:
+            dst[d, req * per] = ST[pl.ds(8 * d, 8), :].astype(BF)
+
+    def ship(d, piece):
         pltpu.make_async_remote_copy(
-            SF.at[d], F.at[me], p2s.at[0], p2r.at[0], device_id=occ_dev(d), device_id_type=MESH).start()
-
-    gather(peer(1), SF, peer(1))
-
-    def answer(k, c):
-        gather(peer(k), SF, peer(k))
-        ship(peer(k - 1))
-        return c
-
-    lax.fori_loop(2, n_occ, answer, 0)
-    ship(peer(n_occ - 1))
-    gather(me, F, me)
-
+            SF.at[d, cut[piece]], F.at[me, cut[piece]], p2s.at[piece], p2r.at[piece],
+            device_id=occ_dev(d), device_id_type=MESH).start()
+
+    def answer_all(piece):
+        gather(peer(1), SF, piece)
+
+        def answer(k, c):
+            gather(peer(k), SF, piece)
+            ship(peer(k - 1), piece)
+            return c
+
+        lax.fori_loop(2, n_occ, answer, 0)
+        ship(peer(n_occ - 1), piece)
+
+    wait_all(RA.at[others], p1r.at[1])
+    answer_all(0)
     for t in range(2):
         firsts[t].wait_recv()
         relays[t].start()
+    wait_all(RZ.at[others], p1r.at[2])
+    RT[...] = RZ[:, n * (per - 1)].astype(F32).reshape(8 * n_occ, 128)
+    answer_all(1)
+    gather(me, F, 0)
+    gather(me, F, 1)
+
     for t in amps:
         t.wait_recv()
     firsts[3].wait_recv()
     near_part(ahead, True)
     firsts[2].wait_recv()
     near_part(behind, True)
-    for t in relays:
-        t.wait_recv()
-    near_part(opposite, True)
-
-    wait_all(F.at[pl.ds(0, n_occ - 1)], p2r.at[0])
+
+    for t in range(2):
+        wait_all(F.at[others, cut[t]], p2r.at[t])
     FT[...] = F[pl.ds(0, n_occ), req * per].astype(F32).reshape(8 * n_occ, 128)
     for j in range(req):
         place(FT[pl.ds(j, npno // 2, stride=8), :], (group + j) // 2, j % 2)
@@ -291,7 +309,7 @@
 
     def block(j, p, a):
         b = ivs[group + 2 * req + rep * n + p, a]
-        return F[pl.ds(ivs[group + j, b], 8), per * j + ivs[group + req + j, b]].reshape(npno, blk)
+        return F[pl.ds(ivs[group + j, b], 8), req * ivs[group + req + j, b] + j].reshape(npno, blk)
 
     z = jnp.zeros((npno, 128), BF)
     for p in range(n):
@@ -327,6 +345,9 @@
 
     rows_in = pl.ds(0, 8 * (n_occ - 1))
     back(BKs, BKr, 0)
+    for t in relays:
+        t.wait_recv()
+    near_part(opposite, True)
     hn = n_occ // 2
     ids = jnp.concatenate(
         [jnp.sum(RQ[pl.ds(h * hn, hn)], axis=0) for h in range(2)], axis=1)
@@ -352,8 +373,10 @@
     for c in firsts + relays + amps:
         c.wait_send()
     wait_all(RQ.at[pl.ds(0, n_occ - 1)], p1s.at[0])
-    wait_all(R1.at[pl.ds(0, n_occ - 1)], p1s.at[1])
-    wait_all(F.at[pl.ds(0, n_occ - 1)], p2s.at[0])
+    wait_all(RA.at[others], p1s.at[1])
+    wait_all(RZ.at[others], p1s.at[2])
+    for t in range(2):
+        wait_all(F.at[others, cut[t]], p2s.at[t])
     wait_all(BKr.at[rows_in], bs.at[0])
     wait_all(BB.at[rows_in], bs.at[1])
 
@@ -379,7 +402,8 @@
         scratch_shapes=[V((n, domb + 1, npno, blk), BF)] * 4 + [
             V((n_occ + 8, req * per + 1, 8, blk), BF),
             V((n_occ, n * per + 1, 8, blk), BF),
-            V((n_occ, n * per + 1, 8, blk), BF),
+            V((n_occ, n, 8, blk), BF),
+            V((n_occ, n * (per - 1) + 1, 8, blk), BF),
             V((n_occ, req * per + 1, 8, blk), BF),
             V((rows, 128), F32),
             V((tiles // 2, 8, 128), BF),
@@ -403,7 +427,7 @@
             V((rows, 128), F32),
             V((rows, 128), F32),
             dma((6,)), dma((6,)), dma((n_rep,)), dma((n_rep,)),
-            dma((2,)), dma((2,)), dma((1,)), dma((1,)), dma((2,)), dma((2,)), dma((4 + n * per,)),
+            dma((3,)), dma((3,)), dma((2,)), dma((2,)), dma((2,)), dma((2,)), dma((4 + n * per,)),
         ],
         compiler_params=pltpu.CompilerParams(
             collective_id=0, has_side_effects=True, vmem_limit_bytes=56 * 1024 * 1024),

time: 58.8 us -> 53.7 us (0.913)
  Pallas kernels: 57 us -> 52 us
    pallas_call x1, Pallas kernels: 57 us -> 52 us  [on_device(): pl.pallas_call(functools.partial(kernel, n_occ, n_rep, n, domb, npno, blk...]
where the time goes in v5:
time: 53.7 us; the launch traced here: 53.4 us
  Pallas kernels  52 us (97%)
  local copies, waits for them, and re-layouts  1.47 us (3%)
    pallas_call x1, Pallas kernels, on_device(): pl.pallas_call(functools.partial(kernel, n_occ, n_rep, n, domb, npno, blk...  52 us
    unnamed x1, local copies, waits for them, and re-layouts  1.47 us

profile of v5, /device:TPU:1, one launch (start us, length us, event | category | flops | bytes accessed | tf_op | source)
XLA Modules:
  0.0 53.4 jit_solution(259002071355722591)
XLA Ops:
  0.0 52.0 %shard_map.82 = f32[4,4096]{1,0:T(4,128)} custom-call(s32[4]{0:T(128)} %cnt.1, s32[2,4]{1,0:T(2,128)} %bitcast.6, s32[2,4]{1,0:T(2,128)} %bitcast.7, bf16[4,12,64,128]{3,2,1,0:T(8,128)(2,1)} %coef.1, bf16[4,3,32,8,128]{4,3,2,1,0:T(8,128)(2,1)} %bitcast.4, bf16[4,4096]{1,0:T(4,128)(2,1)} %amp.1, f32[4,64]{1,0:T(4,128)} %den.1, s32[4,40]{1,0:T(4,128)} %near.1, ...), custom_call_target="tpu_custom_call" | custom-call | tf_op jit(solution)/shard_map/pallas_call | solution.py:397
  52.0 1.5 %copy.10 = f32[4,4096]{1,0:T(4,128)} copy(f32[4,4096]{1,0:T(4,128)} %shard_map.82) | data formatting | bytes 131072

commit v6 on v5

--- a/solution.py
+++ b/solution.py
@@ -32,7 +32,7 @@
     n_occ, n_rep, n, domb, npno, blk, nx, nz,
     cnt, fown, fpair, coef, coefs, amp, den, near, dom,
     out,
-    G0, G1, G2, G3, F, PS, RA, RZ, SF, T0, TP, GP, GT, RT, ST, FT, RR, RQ, rqs, DT, IV, ivs, acc, BD, W,
+    G0, G1, G2, G3, F, PS, RA, RZ, SF, T0, TP, GP, GT, RT, ST, FT, RR, RQ, rqs, DT, IV, ivs, FI, acc, BD, W,
     BKs, BKr, BS, BB, X,
     ysend, yrecv, tsend, trecv, p1s, p1r, p2s, p2r, bs, br, lsem,
 ):
@@ -57,10 +57,6 @@
 
     def at(dx, dz, dc):
         return (lax.rem(mx + dx, nx) * nz + lax.rem(mz + dz, nz)) * cores + lax.rem(mc + dc, cores)
-
-    def peer(k):
-        dx, rest = lax.rem(k, nx), k // nx
-        return at(dx, lax.rem(rest + dx, nz), rest // nz)
 
     def span(d, m):
         return min(d, m - d)
@@ -268,15 +264,14 @@
             device_id=occ_dev(d), device_id_type=MESH).start()
 
     def answer_all(piece):
-        gather(peer(1), SF, piece)
-
-        def answer(k, c):
-            gather(peer(k), SF, piece)
-            ship(peer(k - 1), piece)
-            return c
-
-        lax.fori_loop(2, n_occ, answer, 0)
-        ship(peer(n_occ - 1), piece)
+        last = None
+        for o in outward:
+            d = at(*o)
+            gather(d, SF, piece)
+            if last is not None:
+                ship(last, piece)
+            last = d
+        ship(last, piece)
 
     wait_all(RA.at[others], p1r.at[1])
     answer_all(0)
@@ -296,6 +291,11 @@
     firsts[2].wait_recv()
     near_part(behind, True)
 
+    for j in range(req):
+        for a in range(domb):
+            b = ivs[group + 2 * req + rep * n + j // KN, a]
+            FI[2 * (j * domb + a)] = ivs[group + j, b]
+            FI[2 * (j * domb + a) + 1] = req * ivs[group + req + j, b] + j
     for t in range(2):
         wait_all(F.at[others, cut[t]], p2r.at[t])
     FT[...] = F[pl.ds(0, n_occ), req * per].astype(F32).reshape(8 * n_occ, 128)
@@ -307,15 +307,15 @@
         o = W[slot, pl.ds(1, npno // 2, stride=2), :]
         return jnp.where(lane32, e, pltpu.roll(o, npno, 1))
 
-    def block(j, p, a):
-        b = ivs[group + 2 * req + rep * n + p, a]
-        return F[pl.ds(ivs[group + j, b], 8), req * ivs[group + req + j, b] + j].reshape(npno, blk)
+    def block(j, a):
+        at_ja = 2 * (j * domb + a)
+        return F[pl.ds(FI[at_ja], 8), FI[at_ja + 1]].reshape(npno, blk)
 
     z = jnp.zeros((npno, 128), BF)
     for p in range(n):
         h = jnp.concatenate([G0[p, a] for a in range(domb)], axis=1)
         f = jnp.concatenate([
-            jnp.concatenate([block(j, p, a) for a in range(domb)], axis=1)
+            jnp.concatenate([block(j, a) for a in range(domb)], axis=1)
             for j in range(KN * p, KN * p + KN)], axis=0)
         s = mm_nt(h, f)
         sh, sl = split(s)
@@ -418,6 +418,7 @@
             V((domains.shape[0], domb + -domb % 8), i32),
             V((2 * group + 2 * req, 128), i32),
             pltpu.SMEM((2 * group + 2 * req, 128), i32),
+            pltpu.SMEM((2 * req * domb,), i32),
             V((n * npno, n * npno), F32),
             V((group // 2 + n, 128, 128), F32),
             V((2 * req + n, npno, 128), F32),

time: 53.7 us -> 52.9 us (0.985)
  Pallas kernels: 52 us -> 51.2 us
    pallas_call x1, Pallas kernels: 52 us -> 51.2 us  [on_device(): pl.pallas_call(functools.partial(kernel, n_occ, n_rep, n, domb, npno, blk...]
where the time goes in v6:
time: 52.9 us; the launch traced here: 52.7 us
  Pallas kernels  51.2 us (97%)
  local copies, waits for them, and re-layouts  1.47 us (3%)
    pallas_call x1, Pallas kernels, on_device(): pl.pallas_call(functools.partial(kernel, n_occ, n_rep, n, domb, npno, blk...  51.2 us
    unnamed x1, local copies, waits for them, and re-layouts  1.47 us

profile of v6, /device:TPU:1, one launch (start us, length us, event | category | flops | bytes accessed | tf_op | source)
XLA Modules:
  0.0 52.7 jit_solution(16054727127886923787)
XLA Ops:
  0.0 51.2 %shard_map.82 = f32[4,4096]{1,0:T(4,128)} custom-call(s32[4]{0:T(128)} %cnt.1, s32[2,4]{1,0:T(2,128)} %bitcast.6, s32[2,4]{1,0:T(2,128)} %bitcast.7, bf16[4,12,64,128]{3,2,1,0:T(8,128)(2,1)} %coef.1, bf16[4,3,32,8,128]{4,3,2,1,0:T(8,128)(2,1)} %bitcast.4, bf16[4,4096]{1,0:T(4,128)(2,1)} %amp.1, f32[4,64]{1,0:T(4,128)} %den.1, s32[4,40]{1,0:T(4,128)} %near.1, ...), custom_call_target="tpu_custom_call" | custom-call | tf_op jit(solution)/shard_map/pallas_call | solution.py:397
  51.2 1.5 %copy.10 = f32[4,4096]{1,0:T(4,128)} copy(f32[4,4096]{1,0:T(4,128)} %shard_map.82) | data formatting | bytes 131072

commit v7 on v6

--- a/solution.py
+++ b/solution.py
@@ -32,7 +32,7 @@
     n_occ, n_rep, n, domb, npno, blk, nx, nz,
     cnt, fown, fpair, coef, coefs, amp, den, near, dom,
     out,
-    G0, G1, G2, G3, F, PS, RA, RZ, SF, T0, TP, GP, GT, RT, ST, FT, RR, RQ, rqs, DT, IV, ivs, FI, acc, BD, W,
+    G0, G1, G2, G3, F, PS, RA, RZ, SF, T0, TP, GP, GT, RT, ST, FT, RR, RQ, rqs, DT, IV, ivs, FI, acc, BD, SS, W,
     BKs, BKr, BS, BB, X,
     ysend, yrecv, tsend, trecv, p1s, p1r, p2s, p2r, bs, br, lsem,
 ):
@@ -298,10 +298,6 @@
             FI[2 * (j * domb + a) + 1] = req * ivs[group + req + j, b] + j
     for t in range(2):
         wait_all(F.at[others, cut[t]], p2r.at[t])
-    FT[...] = F[pl.ds(0, n_occ), req * per].astype(F32).reshape(8 * n_occ, 128)
-    for j in range(req):
-        place(FT[pl.ds(j, npno // 2, stride=8), :], (group + j) // 2, j % 2)
-
     def flat(slot):
         e = W[slot, pl.ds(0, npno // 2, stride=2), :]
         o = W[slot, pl.ds(1, npno // 2, stride=2), :]
@@ -320,8 +316,7 @@
         s = mm_nt(h, f)
         sh, sl = split(s)
         th, tl = split(s.T)
-        bd = BD[group // 2 + p].astype(BF)
-        u = mm(jnp.concatenate([sh, sl], axis=1), jnp.concatenate([bd, bd], axis=0))
+        SS[p] = s
         odd = p % 2
         tp = BD[p // 2, pl.ds(odd * npno, npno), :].astype(BF)
         v = mm(jnp.concatenate([tp, tp], axis=1),
@@ -330,8 +325,6 @@
         b = mm(th, vh) + mm(tl, vh) + mm(th, vl)
         W[KN * p, :, :] = b[:npno]
         W[KN * p + 1, :, :] = pltpu.roll(b[npno:], npno, 1)
-        uh, ul = split(u)
-        W[2 * req + p, :, pl.ds(0, npno)] += mm_nt(uh, sh) + mm_nt(ul, sh) + mm_nt(uh, sl)
     for j in range(req):
         BKs[pl.ds(j, npno // 2, stride=8), :] = flat(j)
 
@@ -345,6 +338,15 @@
 
     rows_in = pl.ds(0, 8 * (n_occ - 1))
     back(BKs, BKr, 0)
+    FT[...] = F[pl.ds(0, n_occ), req * per].astype(F32).reshape(8 * n_occ, 128)
+    for j in range(req):
+        place(FT[pl.ds(j, npno // 2, stride=8), :], (group + j) // 2, j % 2)
+    for p in range(n):
+        sh, sl = split(SS[p])
+        bd = BD[group // 2 + p].astype(BF)
+        u = mm(jnp.concatenate([sh, sl], axis=1), jnp.concatenate([bd, bd], axis=0))
+        uh, ul = split(u)
+        W[2 * req + p, :, pl.ds(0, npno)] += mm_nt(uh, sh) + mm_nt(ul, sh) + mm_nt(uh, sl)
     for t in relays:
         t.wait_recv()
     near_part(opposite, True)
@@ -352,6 +354,10 @@
     ids = jnp.concatenate(
         [jnp.sum(RQ[pl.ds(h * hn, hn)], axis=0) for h in range(2)], axis=1)
     hot = (lax.broadcasted_iota(jnp.int32, (8 * n_occ, req * n_occ), 0) == ids).astype(F32).astype(BF)
+    wait_all(BKr.at[rows_in], br.at[0])
+    kh, kl = split(BKr[...])
+    BS[...] = mm(hot, kh) + mm(hot, kl)
+    back(BS, BB, 1)
     for p in range(n):
         X[pl.ds(p, npno // 2, stride=8), :] = flat(2 * req + p)
     de = jnp.concatenate([den[...], jnp.zeros((8 - n, npno), F32)], axis=0)
@@ -360,10 +366,6 @@
         r = pl.ds(8 * i, 8)
         da = jnp.where(low, de[:, 2 * i : 2 * i + 1], de[:, 2 * i + 1 : 2 * i + 2])
         X[r, :] = (da + db) * T0[r, :] + X[r, :]
-    wait_all(BKr.at[rows_in], br.at[0])
-    kh, kl = split(BKr[...])
-    BS[...] = mm(hot, kh) + mm(hot, kl)
-    back(BS, BB, 1)
     wait_all(BB.at[rows_in], br.at[1])
     for i in range(tiles):
         r = pl.ds(8 * i, 8)
@@ -421,6 +423,7 @@
             pltpu.SMEM((2 * req * domb,), i32),
             V((n * npno, n * npno), F32),
             V((group // 2 + n, 128, 128), F32),
+            V((n, npno, KN * npno), F32),
             V((2 * req + n, npno, 128), F32),
             V((rows, 128), F32),
             V((rows, 128), F32),

time: 52.9 us -> 52.7 us (level)
  no operation moved by 1% of the time
where the time goes in v7:
time: 52.7 us; the launch traced here: 52.5 us
  Pallas kernels  51 us (97%)
  local copies, waits for them, and re-layouts  1.47 us (3%)
    pallas_call x1, Pallas kernels, on_device(): pl.pallas_call(functools.partial(kernel, n_occ, n_rep, n, domb, npno, blk...  51 us
    unnamed x1, local copies, waits for them, and re-layouts  1.47 us

profile of v7, /device:TPU:1, one launch (start us, length us, event | category | flops | bytes accessed | tf_op | source)
XLA Modules:
  0.0 52.5 jit_solution(12941143686356074473)
XLA Ops:
  0.0 51.0 %shard_map.82 = f32[4,4096]{1,0:T(4,128)} custom-call(s32[4]{0:T(128)} %cnt.1, s32[2,4]{1,0:T(2,128)} %bitcast.6, s32[2,4]{1,0:T(2,128)} %bitcast.7, bf16[4,12,64,128]{3,2,1,0:T(8,128)(2,1)} %coef.1, bf16[4,3,32,8,128]{4,3,2,1,0:T(8,128)(2,1)} %bitcast.4, bf16[4,4096]{1,0:T(4,128)(2,1)} %amp.1, f32[4,64]{1,0:T(4,128)} %den.1, s32[4,40]{1,0:T(4,128)} %near.1, ...), custom_call_target="tpu_custom_call" | custom-call | tf_op jit(solution)/shard_map/pallas_call | solution.py:399
  51.0 1.5 %copy.10 = f32[4,4096]{1,0:T(4,128)} copy(f32[4,4096]{1,0:T(4,128)} %shard_map.82) | data formatting | bytes 131072
